TPU v7x, 32 devices: a whole 2x2x4 slice. The times are simulated.
32 devices in a mesh: dp: 8 (over z, y), ctx: 4 (over x, core).
Axes of the slice: x: 2, y: 2, z: 4, core: 2. Of those that a mesh axis runs over, the one named last changes fastest.
Arguments:
- tokens: bfloat16 [8, 1024, 1024], P('dp', 'ctx'), may hold values from -6 to 6
- doc_ids: int32 [8, 1024], P('dp', 'ctx'), may hold values from 0 to 7, never falling along the last dimension, each value on 1 to 512 neighbouring positions
- w_query: bfloat16 [1024, 1024], P(('dp', 'ctx')), may hold values from -0.1875 to 0.1875
- key_weight: bfloat16 [1024, 512], P(('dp', 'ctx')), may hold values from -0.1875 to 0.1875
- value_weight: bfloat16 [1024, 512], P(('dp', 'ctx')), may hold values from -0.1875 to 0.1875
- w_output: bfloat16 [1024, 1024], P(None, ('dp', 'ctx')), may hold values from -1.5 to 1.5
- w_gate: bfloat16 [1024, 4608], P(('dp', 'ctx')), may hold values from -0.1875 to 0.1875
- w_up: bfloat16 [1024, 4608], P(('dp', 'ctx')), may hold values from -0.1875 to 0.1875
- w_down: bfloat16 [4608, 1024], P(None, ('dp', 'ctx')), may hold values from -0.09375 to 0.09375
- norm_gains: bfloat16 [2, 1024], P(None, ('dp', 'ctx')), may hold values from 0.5 to 1.5
- head_norm_gains: bfloat16 [2, 64], replicated, may hold values from 0.5 to 1.5
- out_grad: bfloat16 [8, 1024, 1024], P('dp', 'ctx'), may hold values from -6 to 6
Outputs:
- layer_out: bfloat16 [8, 1024, 1024], P('dp', 'ctx')
- input_grad: bfloat16 [8, 1024, 1024], P('dp', 'ctx')
- grad_query: bfloat16 [1024, 1024], P(('dp', 'ctx'))
- grad_key: bfloat16 [1024, 512], P(('dp', 'ctx'))
- grad_value: bfloat16 [1024, 512], P(('dp', 'ctx'))
- grad_output: bfloat16 [1024, 1024], P(None, ('dp', 'ctx'))
- grad_gate: bfloat16 [1024, 4608], P(('dp', 'ctx'))
- grad_up: bfloat16 [1024, 4608], P(('dp', 'ctx'))
- grad_down: bfloat16 [4608, 1024], P(None, ('dp', 'ctx'))
- grad_norms: bfloat16 [2, 1024], P(None, ('dp', 'ctx'))
- grad_heads: bfloat16 [2, 64], replicated
Inputs may be any that keep to these rules, and one draw needn't show every extreme that they name: `doc_ids`: along each sequence the numbers never fall; each document spans 1 to 512 tokens.
All inputs are finite; a program needn't handle non-finite values.
Results may differ from a plain program's by a relative error of at most 0.015.
Values may be sent and summed in bfloat16 or wider, within the bound.
No kernel may reach another device: no remote copies, remote signals or barrier semaphores. Data moves between devices by JAX's collectives and lax.ppermute only.
A program may use at most 320 MiB of HBM per device.

v0:
```python
import math
import jax
import jax.numpy as jnp
from jax import lax
from jax.sharding import PartitionSpec as P

EPS = 1e-05
THETA = 1000000.0
BF = jnp.bfloat16
F32 = jnp.float32
ALL = ("dp", "ctx")


def add_low(a, b):
    return (a.astype(F32) + b.astype(F32)).astype(BF)


def flip(value, axis, size, bits):
    return lax.ppermute(value, axis, [(i, i ^ bits) for i in range(size)])


def gather_ctx(own):
    core = flip(own, "ctx", 4, 1)
    across = flip(own, "ctx", 4, 2)
    return [own, core, across, flip(across, "ctx", 4, 1)]


def scatter_ctx(parts):
    far = flip(parts[3], "ctx", 4, 1)
    near = flip(parts[1], "ctx", 4, 1)
    far_sum = add_low(parts[2], far)
    far_in = flip(far_sum, "ctx", 4, 2)
    return parts[0].astype(F32) + near.astype(F32) + far_in.astype(F32)


def exchange_ctx(parts):
    return [parts[0]] + [flip(parts[j], "ctx", 4, j) for j in range(1, 4)]


def place(parts, where, axis):
    size = parts[0].shape[axis]
    shape = list(parts[0].shape)
    shape[axis] = size * len(parts)
    out = jnp.zeros(shape, parts[0].dtype)
    for part, at in zip(parts, where):
        out = lax.dynamic_update_slice_in_dim(out, part, at * size, axis)
    return out


def ring(value, size):
    return lax.ppermute(value, "dp", [(i, (i + 2) % size) for i in range(size)])


def gather_dp(block, size):
    if size < 4 or size > 8:
        return lax.all_gather(block, "dp", axis=0, tiled=True)
    me = lax.axis_index("dp")
    parts, where = ([], [])
    for step in range(size // 2):
        at = (me - 2 * step) % size
        parts += [block, flip(block, "dp", size, 1)]
        where += [at, at ^ 1]
        if step + 1 < size // 2:
            block = ring(block, size)
    return place(parts, where, 0)


def scatter_dp(whole, size):
    if size < 4 or size > 8:
        return lax.psum_scatter(whole, "dp", scatter_dimension=0, tiled=True).astype(F32)
    me = lax.axis_index("dp")
    rows = whole.shape[0] // size

    def part(at):
        return lax.dynamic_slice_in_dim(whole, at * rows, rows, 0)

    total = None
    for step in range(size // 2):
        at = (me - 2 * (step + 1)) % size
        near = flip(part(at ^ 1), "dp", size, 1)
        own = part(at).astype(F32) + near.astype(F32)
        if total is not None:
            own = own + ring(total, size).astype(F32)
        total = own.astype(BF)
    return own


def sum_all(value, dp_size):
    for bits in (1, 2):
        value = value + flip(value, "ctx", 4, bits)
    bits = 1
    while bits < dp_size:
        value = value + flip(value, "dp", dp_size, bits)
        bits *= 2
    return value


def dot(a, b):
    return lax.dot_general(a, b, (((1,), (0,)), ((), ())), preferred_element_type=F32)


def dot_nt(a, b):
    return lax.dot_general(a, b, (((1,), (1,)), ((), ())), preferred_element_type=F32)


def dot_tn(a, b):
    return lax.dot_general(a, b, (((0,), (0,)), ((), ())), preferred_element_type=F32)


def rms_scale(values, gain_row):
    return values * lax.rsqrt(jnp.mean(values * values, -1, keepdims=True) + EPS) * gain_row


def rope_tables(positions, width_all):
    half_width = width_all // 2
    freqs = THETA ** (-(2.0 * jnp.arange(half_width, dtype=jnp.float32)) / width_all)
    angles = positions.astype(jnp.float32)[..., None] * freqs
    angles = jnp.concatenate([angles, angles], -1)
    return (jnp.cos(angles), jnp.sin(angles))


def rotate(values, cosine_table, sine_table):
    half_width = values.shape[-1] // 2
    turned = jnp.concatenate([-values[..., half_width:], values[..., :half_width]], -1)
    return values * cosine_table + turned * sine_table


def head_prepare(projected, gain_row, cosine_table, sine_table, head_count):
    shaped = projected.reshape(projected.shape[:-1] + (head_count, gain_row.shape[0]))
    normed = rms_scale(shaped, gain_row)
    return rotate(normed, cosine_table[..., None, :], sine_table[..., None, :])


def split_parts(tall, count):
    rows = tall.shape[0] // count
    return [lax.slice_in_dim(tall, j * rows, (j + 1) * rows, axis=0) for j in range(count)]


def on_device(
    dp_size,
    tokens,
    doc_ids,
    w_query,
    key_weight,
    value_weight,
    w_output,
    w_gate,
    w_up,
    w_down,
    norm_gains,
    head_norm_gains,
    out_grad,
):
    local_len, model_dim = tokens.shape[1:]
    tokens, out_grad, doc_row = (tokens[0], out_grad[0], doc_ids[0])
    head_dim = head_norm_gains.shape[1]
    q_cols, kv_cols = (w_query.shape[1] // 4, key_weight.shape[1] // 4)
    q_heads, kv_heads = (q_cols // head_dim, kv_cols // head_dim)
    group_size = q_heads // kv_heads
    scale_by = 1.0 / math.sqrt(head_dim)
    shard = norm_gains.shape[1]
    ff_cols = w_gate.shape[1] // 4
    me = lax.axis_index("ctx")
    places = [me ^ j for j in range(4)]

    def spread(pieces):
        sent = []
        for at in places:
            cut = [
                lax.dynamic_slice_in_dim(p, at * (p.shape[1] // 4), p.shape[1] // 4, 1)
                for p in pieces
            ]
            sent.append(jnp.concatenate(cut, 1))
        block = place(exchange_ctx(sent), places, 0)
        return gather_dp(block, dp_size)

    gains_full = lax.all_gather(norm_gains, ALL, axis=1, tiled=True).astype(F32)
    attn_w = spread([w_query, key_weight, value_weight, w_output.T])
    wq = attn_w[:, :q_cols]
    wk = attn_w[:, q_cols : q_cols + kv_cols]
    wv = attn_w[:, q_cols + kv_cols : q_cols + 2 * kv_cols]
    wo_t = attn_w[:, q_cols + 2 * kv_cols :]
    wg = spread([w_gate])
    wu = spread([w_up])
    wd_t = spread([w_down.T])
    head_full = head_norm_gains.astype(F32)
    docs = jnp.concatenate(gather_ctx(doc_row.reshape(1, -1)), 1)[0]
    all_tokens = jnp.concatenate(gather_ctx(tokens), 0)
    all_grad = jnp.concatenate(gather_ctx(out_grad), 0)
    index = jnp.concatenate(
        [at * local_len + jnp.arange(local_len, dtype=jnp.int32) for at in places]
    )
    earlier = jnp.sum((docs[None, :] < docs[:, None]).astype(jnp.int32), -1)
    positions = index - earlier
    visible = (docs[None, :] == docs[:, None]) & (index[None, :] <= index[:, None])
    cosine_table, sine_table = rope_tables(positions, head_dim)
    inputs = all_tokens.astype(F32)
    normed_one = rms_scale(inputs, gains_full[0]).astype(BF)
    q_pre = dot(normed_one, wq)
    k_pre = dot(normed_one, wk)
    value_rows = dot(normed_one, wv).astype(BF)
    query_rows = head_prepare(q_pre, head_full[0], cosine_table, sine_table, q_heads).astype(BF)
    key_rows = head_prepare(k_pre, head_full[1], cosine_table, sine_table, kv_heads).astype(BF)
    value_rows = value_rows.reshape(-1, kv_heads, head_dim)
    grouped = query_rows.reshape(-1, kv_heads, group_size, head_dim)

    def attend_scores():
        raw = jnp.einsum("tkgd,skd->kgts", grouped, key_rows, preferred_element_type=F32) * scale_by
        return jnp.where(visible[None, None], raw, -1e30)

    scores = attend_scores()
    top_row = jnp.max(scores, -1, keepdims=True)
    expd = jnp.exp(scores - top_row)
    total_row = jnp.sum(expd, -1, keepdims=True)
    probs = expd / total_row
    log_total = top_row + jnp.log(total_row)
    mixed = jnp.einsum("kgts,skd->tkgd", probs.astype(BF), value_rows, preferred_element_type=F32)
    attn_out = mixed.reshape(-1, q_cols).astype(BF)
    resid_sum = scatter_ctx(split_parts(dot_nt(attn_out, wo_t).astype(BF), 4))
    resid = tokens.astype(F32) + resid_sum
    normed_own = rms_scale(resid, gains_full[1]).astype(BF)
    normed_two = jnp.concatenate(gather_ctx(normed_own), 0)
    gate_act = dot(normed_two, wg)
    up_act = dot(normed_two, wu)
    hidden = (jax.nn.silu(gate_act) * up_act).astype(BF)
    grad_hidden = dot(all_grad, wd_t)
    _, gate_pull = jax.vjp(lambda g, u: jax.nn.silu(g) * u, gate_act, up_act)
    grad_gate_full, grad_up_full = gate_pull(grad_hidden)
    grad_gate = grad_gate_full.astype(BF)
    grad_up = grad_up_full.astype(BF)
    grad_two_part = (dot_nt(grad_gate, wg) + dot_nt(grad_up, wu)).astype(BF)
    grad_norm_two = scatter_ctx(split_parts(grad_two_part, 4))
    _, second_pull = jax.vjp(rms_scale, resid, gains_full[1])
    grad_resid_norm, grad_gain_two = second_pull(grad_norm_two)
    grad_resid = out_grad.astype(F32) + grad_resid_norm
    down_part = dot_nt(hidden, wd_t).astype(BF)
    layer_out = (resid + scatter_ctx(split_parts(down_part, 4))).astype(BF)

    def collect(whole, widths):
        mine = scatter_dp(whole.astype(BF), dp_size).astype(BF)
        sent = [lax.dynamic_slice_in_dim(mine, at * shard, shard, 0) for at in places]
        got = exchange_ctx(sent)
        outs, start = ([], 0)
        for width in widths:
            cut = [g[:, start : start + width] for g in got]
            outs.append(place(cut, places, 1))
            start += width
        return outs

    (grad_g_out,) = collect(dot_tn(normed_two, grad_gate), (ff_cols,))
    (grad_u_out,) = collect(dot_tn(normed_two, grad_up), (ff_cols,))
    (grad_d_out,) = collect(dot_tn(all_grad, hidden), (ff_cols,))
    grad_attn = jnp.concatenate(gather_ctx(grad_resid.astype(BF)), 0)
    grad_mixed = dot(grad_attn, wo_t).astype(BF)
    grad_grouped = grad_mixed.reshape(-1, kv_heads, group_size, head_dim)
    probs = jnp.exp(attend_scores() - log_total)
    grad_probs = jnp.einsum("tkgd,skd->kgts", grad_grouped, value_rows, preferred_element_type=F32)
    value_part = jnp.einsum(
        "kgts,tkgd->skd", probs.astype(BF), grad_grouped, preferred_element_type=F32
    )
    inner_row = jnp.sum(probs * grad_probs, -1, keepdims=True)
    grad_scores = (probs * (grad_probs - inner_row)).astype(BF)
    grad_queries = (
        jnp.einsum("kgts,skd->tkgd", grad_scores, key_rows, preferred_element_type=F32) * scale_by
    )
    grad_keys = (
        jnp.einsum("kgts,tkgd->skd", grad_scores, grouped, preferred_element_type=F32) * scale_by
    )
    _, query_pull = jax.vjp(
        lambda v, g: head_prepare(v, g, cosine_table, sine_table, q_heads), q_pre, head_full[0]
    )
    grad_q_pre, grad_q_gain = query_pull(grad_queries.reshape(-1, q_heads, head_dim))
    _, key_pull = jax.vjp(
        lambda v, g: head_prepare(v, g, cosine_table, sine_table, kv_heads), k_pre, head_full[1]
    )
    grad_k_pre, grad_k_gain = key_pull(grad_keys)
    grad_qkv = jnp.concatenate(
        [grad_q_pre.astype(BF), grad_k_pre.astype(BF), value_part.reshape(-1, kv_cols).astype(BF)],
        1,
    )
    w_qkv = attn_w[:, : q_cols + 2 * kv_cols]
    grad_one_part = dot_nt(grad_qkv, w_qkv)
    _, first_pull = jax.vjp(rms_scale, inputs, gains_full[0])
    grad_gain_one = first_pull(grad_one_part)[1]
    grad_norm_one = scatter_ctx(split_parts(grad_one_part.astype(BF), 4))
    _, own_pull = jax.vjp(rms_scale, tokens.astype(F32), gains_full[0])
    input_grad = (grad_resid + own_pull(grad_norm_one)[0]).astype(BF)
    grad_attn_w = jnp.concatenate([dot_tn(normed_one, grad_qkv), dot_tn(grad_attn, attn_out)], 1)
    grad_q_out, grad_k_out, grad_v_out, grad_o_out = collect(
        grad_attn_w, (q_cols, kv_cols, kv_cols, q_cols)
    )
    small = jnp.concatenate([grad_gain_one, grad_gain_two, grad_q_gain, grad_k_gain])
    small = sum_all(small.reshape(1, -1), dp_size)[0]
    norm_total = small[: 2 * model_dim].reshape(2, model_dim)
    head_sum = small[2 * model_dim :].reshape(2, head_dim)
    norm_own = lax.dynamic_slice_in_dim(norm_total, lax.axis_index(ALL) * shard, shard, 1)
    return (
        layer_out[None],
        input_grad[None],
        grad_q_out,
        grad_k_out,
        grad_v_out,
        grad_o_out.T,
        grad_g_out,
        grad_u_out,
        grad_d_out.T,
        norm_own.astype(BF),
        head_sum.astype(BF),
    )


def solution(mesh):

    def step(*arrays):
        return on_device(mesh.shape["dp"], *arrays)

    in_specs = (
        P("dp", "ctx", None),
        P("dp", "ctx"),
        P(("dp", "ctx"), None),
        P(("dp", "ctx"), None),
        P(("dp", "ctx"), None),
        P(None, ("dp", "ctx")),
        P(("dp", "ctx"), None),
        P(("dp", "ctx"), None),
        P(None, ("dp", "ctx")),
        P(None, ("dp", "ctx")),
        P(),
        P("dp", "ctx", None),
    )
    out_specs = (
        P("dp", "ctx", None),
        P("dp", "ctx", None),
        P(("dp", "ctx"), None),
        P(("dp", "ctx"), None),
        P(("dp", "ctx"), None),
        P(None, ("dp", "ctx")),
        P(("dp", "ctx"), None),
        P(("dp", "ctx"), None),
        P(None, ("dp", "ctx")),
        P(None, ("dp", "ctx")),
        P(),
    )
    return jax.shard_map(step, mesh=mesh, in_specs=in_specs, out_specs=out_specs, check_vma=False)
```

profile of v0, /device:TPU:0, one launch (start us, length us, event | category | flops | bytes accessed | tf_op | source)
XLA Modules:
  0.0 532.0 jit_solution(6411378108556584978)
XLA Ops:
  1.2 2.6 collective-permute-start.14
  10.2 41.8 %all-gather = bf16[32,32,2]{1,2,0:T(2,128)(2,1)S(1)} all-gather(bf16[1,32,2]{1,2,0:T(2,128)(2,1)} %bitcast.173), channel_id=1, replica_groups=mesh['dp'=8,'ctx'=4] {'dp','ctx'}, dimensions={0}, use_global_device_ids=true | all-gather | bytes 4224 | tf_op jit(solution)/shard_map/all_gather | solution.py:177
  65.7 4.2 collective-permute-done.33
  69.9 4.1 collective-permute-done.34
  79.7 3.5 collective-permute-done.23
  83.2 2.1 collective-permute-start.35
  85.5 5.5 %collective-permute-done.6 = bf16[128,768]{1,0:T(8,128)(2,1)S(1)} collective-permute-done((bf16[128,768]{1,0:T(8,128)(2,1)S(1)}, bf16[128,768]{1,0:T(8,128)(2,1)S(1)}, u32[]{:S(2)}, u32[]{:S(2)}) %collective-permute-start.6) | collective-permute-done | bytes 196640 | tf_op jit(solution)/shard_map/ppermute | solution.py:19
  91.1 4.6 collective-permute-done.35
  96.7 8.2 %collective-permute-done.36 = bf16[128,1152]{1,0:T(8,128)(2,1)S(1)} collective-permute-done((bf16[128,1152]{1,0:T(8,128)(2,1)S(1)}, bf16[128,1152]{1,0:T(8,128)(2,1)S(1)}, u32[]{:S(2)}, u32[]{:S(2)}) %collective-permute-start.36) | collective-permute-done | bytes 294944 | tf_op jit(solution)/shard_map/ppermute | solution.py:51
  106.3 7.9 %collective-permute-done.46 = bf16[128,1152]{1,0:T(8,128)(2,1)S(1)} collective-permute-done((bf16[128,1152]{1,0:T(8,128)(2,1)S(1)}, bf16[128,1152]{1,0:T(8,128)(2,1)S(1)}, u32[]{:S(2)}, u32[]{:S(2)}) %collective-permute-start.46) | collective-permute-done | bytes 294944 | tf_op jit(solution)/shard_map/ppermute | solution.py:51
  114.4 2.1 collective-permute-start.37
  116.5 7.1 %collective-permute-done.9 = bf16[128,768]{1,0:T(8,128)(2,1)S(1)} collective-permute-done((bf16[128,768]{1,0:T(8,128)(2,1)S(1)}, bf16[128,768]{1,0:T(8,128)(2,1)S(1)}, u32[]{:S(2)}, u32[]{:S(2)}) %collective-permute-start.9) | collective-permute-done | bytes 196640 | tf_op jit(solution)/shard_map/ppermute | solution.py:51
  123.6 6.7 %collective-permute-done.10 = bf16[128,768]{1,0:T(8,128)(2,1)S(1)} collective-permute-done((bf16[128,768]{1,0:T(8,128)(2,1)S(1)}, bf16[128,768]{1,0:T(8,128)(2,1)S(1)}, u32[]{:S(2)}, u32[]{:S(2)}) %collective-permute-start.10) | collective-permute-done | bytes 196640 | tf_op jit(solution)/shard_map/ppermute | solution.py:19
  133.3 10.3 %collective-permute-done.38 = bf16[128,1152]{1,0:T(8,128)(2,1)} collective-permute-done((bf16[128,1152]{1,0:T(8,128)(2,1)S(1)}, bf16[128,1152]{1,0:T(8,128)(2,1)}, u32[]{:S(2)}, u32[]{:S(2)}) %collective-permute-start.38) | collective-permute-done | bytes 294944 | tf_op jit(solution)/shard_map/ppermute | solution.py:51
  146.0 6.2 %collective-permute-done.48 = bf16[128,1152]{1,0:T(8,128)(2,1)} collective-permute-done((bf16[128,1152]{1,0:T(8,128)(2,1)S(1)}, bf16[128,1152]{1,0:T(8,128)(2,1)}, u32[]{:S(2)}, u32[]{:S(2)}) %collective-permute-start.48) | collective-permute-done | bytes 294944 | tf_op jit(solution)/shard_map/ppermute | solution.py:51
  153.4 2.0 collective-permute-done.28
  157.2 3.8 collective-permute-done.12
  161.1 5.9 %collective-permute-done.39 = bf16[128,1152]{1,0:T(8,128)(2,1)S(1)} collective-permute-done((bf16[128,1152]{1,0:T(8,128)(2,1)}, bf16[128,1152]{1,0:T(8,128)(2,1)S(1)}, u32[]{:S(2)}, u32[]{:S(2)}) %collective-permute-start.39) | collective-permute-done | bytes 294944 | tf_op jit(solution)/shard_map/ppermute | solution.py:19
  170.3 4.8 fusion.15
  179.5 7.5 %fusion.97 = (f32[2,2,1024]{2,1,0:T(2,128)S(1)}, f32[2,2,1024,1024]{2,3,1,0:T(8,128)}) fusion(bf16[1024,2,64,1]{0,2,3,1:T(8,128)(2,1)S(1)} %fusion.47, bf16[1024,2,2,64]{0,3,2,1:T(8,128)(2,1)S(1)} %fusion.34, pred[1024,1024]{0,1:T(8,128)(4,1)S(1)} %copy-done.26), kind=kOutput, calls=%fused_computation.347 | convolution fusion | flops 549449728 | bytes 18628608 | tf_op jit(solution)/shard_map/tkgd,skd->kgts/dot_general | solution.py:208
  186.9 8.0 %fusion.3 = f32[2,2,1024]{2,1,0:T(2,128)S(1)} fusion(f32[2,2,1024,1024]{2,3,1,0:T(8,128)} %get-tuple-element.138, f32[2,2,1024]{2,1,0:T(2,128)S(1)} %get-tuple-element.137), kind=kLoop, calls=%fused_computation.9 | loop fusion | flops 8384512 | bytes 16809984 | tf_op jit(solution)/shard_map/reduce_sum | solution.py:214
  194.9 7.5 %fusion.18 = bf16[2,64,2,1024]{3,1,2,0:T(8,128)(2,1)S(1)} fusion(bf16[1024,2,64,1]{0,2,3,1:T(8,128)(2,1)S(1)} %bitcast.152, f32[2,2,1024,1024]{2,3,1,0:T(8,128)} %get-tuple-element.138, f32[2,2,1024]{2,1,0:T(2,128)S(1)} %fusion.3, f32[2,2,1024]{2,1,0:T(2,128)S(1)} %get-tuple-element.137), kind=kOutput, calls=%fused_computation.68 | convolution fusion | flops 549715968 | bytes 17596416 | tf_op jit(solution)/shard_map/kgts,skd->tkgd/dot_general | solution.py:217
  206.4 13.0 %collective-permute-start.50 = (bf16[128,1152]{1,0:T(8,128)(2,1)}, bf16[128,1152]{1,0:T(8,128)(2,1)S(1)}, u32[]{:S(2)}, u32[]{:S(2)}) collective-permute-start(bf16[128,1152]{1,0:T(8,128)(2,1)} %collective-permute-done.48), channel_id=1, source_target_pairs={{0,8},{4,12},{8,16},{12,20},{16,24},{20,28},{24,0},{28,4},{1,9},{5... | collective-permute-start | bytes 884744 | tf_op jit(solution)/shard_map/ppermute | solution.py:51
  221.2 9.1 %collective-permute-done.50 = bf16[128,1152]{1,0:T(8,128)(2,1)S(1)} collective-permute-done((bf16[128,1152]{1,0:T(8,128)(2,1)}, bf16[128,1152]{1,0:T(8,128)(2,1)S(1)}, u32[]{:S(2)}, u32[]{:S(2)}) %collective-permute-start.50) | collective-permute-done | bytes 294944 | tf_op jit(solution)/shard_map/ppermute | solution.py:51
  232.5 2.7 collective-permute-done.18
  236.5 15.1 %collective-permute-done.41 = bf16[128,1152]{1,0:T(8,128)(2,1)S(1)} collective-permute-done((bf16[128,1152]{1,0:T(8,128)(2,1)}, bf16[128,1152]{1,0:T(8,128)(2,1)S(1)}, u32[]{:S(2)}, u32[]{:S(2)}) %collective-permute-start.41) | collective-permute-done | bytes 294944 | tf_op jit(solution)/shard_map/ppermute | solution.py:19
  252.9 11.4 %collective-permute-done.20 = bf16[256,1024]{1,0:T(8,128)(2,1)S(1)} collective-permute-done((bf16[256,1024]{1,0:T(8,128)(2,1)S(1)}, bf16[256,1024]{1,0:T(8,128)(2,1)S(1)}, u32[]{:S(2)}, u32[]{:S(2)}) %collective-permute-start.20) | collective-permute-done | bytes 524320 | tf_op jit(solution)/shard_map/ppermute | solution.py:19
  264.4 4.4 fusion.46
  268.8 4.5 fusion.77
  273.3 8.2 %fusion.13 = (bf16[1024,1152]{1,0:T(8,128)(2,1)}, bf16[1024,1152]{1,0:T(8,128)(2,1)}, bf16[1024,1152]{1,0:T(8,128)(2,1)S(1)}) fusion(f32[1024,1152]{1,0:T(8,128)S(1)} %fusion.46, f32[1024,1152]{1,0:T(8,128)S(1)} %fusion.77, bf16[1024,1152]{1,0:T(8,128)(2,1)S(1)} %constant_dynamic-update-slice_fusion.47, bf16[256,1024]{1,0:T(8,128)(2,1)S(1)} %collective-permute-done.21, ...), kind=kOutput, calls=%fused_computation.21 | convolution fusion | flops 2443182080 | bytes 20971520 | tf_op jit(solution)/shard_map/dot_general | solution.py:99
  281.5 3.1 convolution_convert_fusion.3
  285.4 4.4 convolution_convert_fusion
  292.3 4.6 fusion.98
  296.9 3.2 convolution_convert_fusion.1
  301.7 3.1 add_convert_fusion
  304.9 3.4 convolution_convert_fusion.2
  310.4 7.9 %collective-permute-done.90 = bf16[128,1152]{1,0:T(8,128)(2,1)S(1)} collective-permute-done((bf16[128,1152]{1,0:T(8,128)(2,1)S(1)}, bf16[128,1152]{1,0:T(8,128)(2,1)S(1)}, u32[]{:S(2)}, u32[]{:S(2)}) %collective-permute-start.90) | collective-permute-done | bytes 294944 | tf_op jit(solution)/shard_map/ppermute | solution.py:19
  318.9 8.0 %collective-permute-done.80 = bf16[128,1152]{1,0:T(8,128)(2,1)S(1)} collective-permute-done((bf16[128,1152]{1,0:T(8,128)(2,1)S(1)}, bf16[128,1152]{1,0:T(8,128)(2,1)S(1)}, u32[]{:S(2)}, u32[]{:S(2)}) %collective-permute-start.80) | collective-permute-done | bytes 294944 | tf_op jit(solution)/shard_map/ppermute | solution.py:19
  329.5 8.7 %collective-permute-done.101 = bf16[128,1152]{1,0:T(8,128)(2,1)S(1)} collective-permute-done((bf16[128,1152]{1,0:T(8,128)(2,1)S(1)}, bf16[128,1152]{1,0:T(8,128)(2,1)S(1)}, u32[]{:S(2)}, u32[]{:S(2)}) %collective-permute-start.101) | collective-permute-done | bytes 294944 | tf_op jit(solution)/shard_map/ppermute | solution.py:51
  338.8 9.9 %collective-permute-done.91 = bf16[128,1152]{1,0:T(8,128)(2,1)S(1)} collective-permute-done((bf16[128,1152]{1,0:T(8,128)(2,1)S(1)}, bf16[128,1152]{1,0:T(8,128)(2,1)S(1)}, u32[]{:S(2)}, u32[]{:S(2)}) %collective-permute-start.91) | collective-permute-done | bytes 294944 | tf_op jit(solution)/shard_map/ppermute | solution.py:51
  349.2 9.1 %collective-permute-done.81 = bf16[128,1152]{1,0:T(8,128)(2,1)S(1)} collective-permute-done((bf16[128,1152]{1,0:T(8,128)(2,1)S(1)}, bf16[128,1152]{1,0:T(8,128)(2,1)S(1)}, u32[]{:S(2)}, u32[]{:S(2)}) %collective-permute-start.81) | collective-permute-done | bytes 294944 | tf_op jit(solution)/shard_map/ppermute | solution.py:51
  358.8 8.1 %collective-permute-done.102 = bf16[128,1152]{1,0:T(8,128)(2,1)S(1)} collective-permute-done((bf16[128,1152]{1,0:T(8,128)(2,1)S(1)}, bf16[128,1152]{1,0:T(8,128)(2,1)S(1)}, u32[]{:S(2)}, u32[]{:S(2)}) %collective-permute-start.102) | collective-permute-done | bytes 294944 | tf_op jit(solution)/shard_map/ppermute | solution.py:51
  367.4 8.0 %collective-permute-done.92 = bf16[128,1152]{1,0:T(8,128)(2,1)S(1)} collective-permute-done((bf16[128,1152]{1,0:T(8,128)(2,1)S(1)}, bf16[128,1152]{1,0:T(8,128)(2,1)S(1)}, u32[]{:S(2)}, u32[]{:S(2)}) %collective-permute-start.92) | collective-permute-done | bytes 294944 | tf_op jit(solution)/shard_map/ppermute | solution.py:51
  375.9 8.0 %collective-permute-done.82 = bf16[128,1152]{1,0:T(8,128)(2,1)S(1)} collective-permute-done((bf16[128,1152]{1,0:T(8,128)(2,1)S(1)}, bf16[128,1152]{1,0:T(8,128)(2,1)S(1)}, u32[]{:S(2)}, u32[]{:S(2)}) %collective-permute-start.82) | collective-permute-done | bytes 294944 | tf_op jit(solution)/shard_map/ppermute | solution.py:51
  387.0 7.3 %collective-permute-done.54 = bf16[256,1024]{1,0:T(8,128)(2,1)S(1)} collective-permute-done((bf16[256,1024]{1,0:T(8,128)(2,1)S(1)}, bf16[256,1024]{1,0:T(8,128)(2,1)S(1)}, u32[]{:S(2)}, u32[]{:S(2)}) %collective-permute-start.54) | collective-permute-done | bytes 524320 | tf_op jit(solution)/shard_map/ppermute | solution.py:19
  394.3 2.5 fusion.80
  400.8 2.9 collective-permute-done.93
  408.9 2.2 collective-permute-done.105
  411.1 2.5 collective-permute-start.95
  415.9 2.0 collective-permute-start.85
  424.3 3.9 fusion.22
  428.2 8.5 %fusion = (f32[2,2,1024]{2,1,0:T(2,128)S(1)}, f32[2,1024,1024,2]{2,1,3,0:T(8,128)}) fusion(f32[2,2,1024,1024]{2,3,1,0:T(8,128)S(1)} %bitcast.139, f32[2,2,1024]{2,1,0:T(2,128)S(1)} %log_add_fusion, bf16[1024,2,64,1]{0,2,3,1:T(8,128)(2,1)} %bitcast.153, bf16[1024,2,2,64]{0,3,2,1:T(8,128)(2,1)S(1)} %bitcast.149), kind=kOutput, calls=%fused_computation.2 | convolution fusion | flops 549449728 | bytes 34373632 | tf_op jit(solution)/shard_map/tkgd,skd->kgts/dot_general | solution.py:257
  436.7 8.3 %fusion.2 = bf16[2,2,1024,1024]{2,3,1,0:T(8,128)(2,1)S(1)} fusion(f32[2,1024,1024,2]{2,1,3,0:T(8,128)} %get-tuple-element.140, f32[2,2,1024,1024]{2,3,1,0:T(8,128)S(1)} %bitcast.139, f32[2,2,1024]{2,1,0:T(2,128)S(1)} %get-tuple-element.139, f32[2,2,1024]{2,1,0:T(2,128)S(1)} %log_add_fusion), kind=kLoop, calls=%fused_computation.4 | loop fusion | flops 16777216 | bytes 41975808 | tf_op jit(solution)/shard_map/convert_element_type | solution.py:262
  448.4 6.1 %broadcast_multiply_fusion = (f32[1024,2,64]{0,2,1:T(8,128)S(1)}, f32[1024,2,64]{0,2,1:T(8,128)S(1)}) fusion(f32[1024,64]{0,1:T(8,128)S(1)} %copy-done.16, bf16[1024,2,2,64]{0,3,2,1:T(8,128)(2,1)S(1)} %copy-done.18, bf16[2,2,1024,1024]{2,3,1,0:T(8,128)(2,1)} %copy-done), kind=kOutput, calls=%fused_computation.148 | convolution fusion | flops 537001984 | bytes 10223616 | tf_op jit(solution)/shard_map/kgts,tkgd->skd/dot_general | solution.py:267
  458.6 4.3 fusion.16
  463.2 2.2 convolution_convert_fusion.6
  476.7 2.8 collective-permute-start.111
  483.3 5.9 %collective-permute-done.69 = bf16[128,768]{0,1:T(8,128)(2,1)} collective-permute-done((bf16[128,768]{0,1:T(8,128)(2,1)}, bf16[128,768]{0,1:T(8,128)(2,1)}, u32[]{:S(2)}, u32[]{:S(2)}) %collective-permute-start.69) | collective-permute-done | bytes 196640 | tf_op jit(solution)/shard_map/ppermute | solution.py:19
  492.9 7.6 %collective-permute-done.72 = bf16[128,768]{0,1:T(8,128)(2,1)} collective-permute-done((bf16[128,768]{0,1:T(8,128)(2,1)}, bf16[128,768]{0,1:T(8,128)(2,1)}, u32[]{:S(2)}, u32[]{:S(2)}) %collective-permute-start.72) | collective-permute-done | bytes 196640 | tf_op jit(solution)/shard_map/ppermute | solution.py:51
  501.5 2.2 add_convert_fusion.1
  504.9 5.0 collective-permute-done.73
  512.8 8.9 %collective-permute-done.76 = bf16[32,768]{0,1:T(8,128)(2,1)S(1)} collective-permute-done((bf16[32,768]{0,1:T(8,128)(2,1)S(1)}, bf16[32,768]{0,1:T(8,128)(2,1)S(1)}, u32[]{:S(2)}, u32[]{:S(2)}) %collective-permute-start.76) | collective-permute-done | bytes 49184 | tf_op jit(solution)/shard_map/ppermute | solution.py:19
  521.6 4.3 collective-permute-done.75
  529.2 2.6 fusion.39
  (512 shorter events, 122.7 us)
Async XLA Ops:
  0.7 56.2 %collective-permute-start.13 = (s32[1,256]{1,0:T(1,128)}, s32[1,256]{1,0:T(1,128)S(1)}, u32[]{:S(2)}, u32[]{:S(2)}) collective-permute-start(s32[1,256]{1,0:T(1,128)} %param.13), channel_id=1, source_target_pairs={{0,1},{1,0},{2,3},{3,2},{4,5},{5,4},{6,7},{7,6},{8,9},{9,8},{10,11... | collective-permute-start | bytes 3080 | tf_op jit(solution)/shard_map/ppermute | solution.py:19
  1.2 55.3 %collective-permute-start.14 = (s32[1,256]{1,0:T(1,128)}, s32[1,256]{1,0:T(1,128)S(1)}, u32[]{:S(2)}, u32[]{:S(2)}) collective-permute-start(s32[1,256]{1,0:T(1,128)} %param.13), channel_id=1, source_target_pairs={{0,2},{1,3},{2,0},{3,1},{4,6},{5,7},{6,4},{7,5},{8,10},{9,11},{10,... | collective-permute-start | bytes 3080 | tf_op jit(solution)/shard_map/ppermute | solution.py:19
  3.7 141.6 %collective-permute-start.1 = (bf16[256,1024]{1,0:T(8,128)(2,1)}, bf16[256,1024]{1,0:T(8,128)(2,1)S(1)}, u32[]{:S(2)}, u32[]{:S(2)}) collective-permute-start(bf16[256,1024]{1,0:T(8,128)(2,1)} %bitcast.143), channel_id=1, source_target_pairs={{0,2},{1,3},{2,0},{3,1},{4,6},{5,7},{6,4},{7,5},{8,10},{9,11},{10,... | collective-permute-start | bytes 1572872 | tf_op jit(solution)/shard_map/ppermute | solution.py:19
  3.8 164.2 %collective-permute-start = (bf16[256,1024]{1,0:T(8,128)(2,1)}, bf16[256,1024]{1,0:T(8,128)(2,1)S(1)}, u32[]{:S(2)}, u32[]{:S(2)}) collective-permute-start(bf16[256,1024]{1,0:T(8,128)(2,1)} %bitcast.144), channel_id=1, source_target_pairs={{0,1},{1,0},{2,3},{3,2},{4,5},{5,4},{6,7},{7,6},{8,9},{9,8},{10,11... | collective-permute-start | bytes 1572872 | tf_op jit(solution)/shard_map/ppermute | solution.py:19
  7.6 56.2 %collective-permute-start.4 = (bf16[32,768]{1,0:T(8,128)(2,1)}, bf16[32,768]{1,0:T(8,128)(2,1)S(1)}, u32[]{:S(2)}, u32[]{:S(2)}) collective-permute-start(bf16[32,768]{1,0:T(8,128)(2,1)} %pad_maximum_fusion.13), channel_id=1, source_target_pairs={{0,2},{1,3},{2,0},{3,1},{4,6},{5,7},{6,4},{7,5},{8,10},{9,11},{10,... | collective-permute-start | bytes 147464 | tf_op jit(solution)/shard_map/ppermute | solution.py:19
  62.0 16.7 %collective-permute-start.44 = (bf16[32,1152]{1,0:T(8,128)(2,1)S(1)}, bf16[32,1152]{1,0:T(8,128)(2,1)S(1)}, u32[]{:S(2)}, u32[]{:S(2)}) collective-permute-start(bf16[32,1152]{1,0:T(8,128)(2,1)S(1)} %get-tuple-element.75), channel_id=1, source_target_pairs={{0,3},{1,2},{2,1},{3,0},{4,7},{5,6},{6,5},{7,4},{8,11},{9,10},{10,... | collective-permute-start | bytes 221192 | tf_op jit(solution)/shard_map/ppermute | solution.py:19
  63.8 13.0 %collective-permute-start.42 = (bf16[32,1152]{1,0:T(8,128)(2,1)S(1)}, bf16[32,1152]{1,0:T(8,128)(2,1)S(1)}, u32[]{:S(2)}, u32[]{:S(2)}) collective-permute-start(bf16[32,1152]{1,0:T(8,128)(2,1)S(1)} %get-tuple-element.76), channel_id=1, source_target_pairs={{0,1},{1,0},{2,3},{3,2},{4,5},{5,4},{6,7},{7,6},{8,9},{9,8},{10,11... | collective-permute-start | bytes 221192 | tf_op jit(solution)/shard_map/ppermute | solution.py:19
  79.7 11.4 %collective-permute-start.7 = (bf16[128,768]{1,0:T(8,128)(2,1)S(1)}, bf16[128,768]{1,0:T(8,128)(2,1)S(1)}, u32[]{:S(2)}, u32[]{:S(2)}) collective-permute-start(bf16[128,768]{1,0:T(8,128)(2,1)S(1)} %constant_dynamic-update-slice_fusion.66), channel_id=1, source_target_pairs={{0,8},{4,12},{8,16},{12,20},{16,24},{20,28},{24,0},{28,4},{1,9},{5... | collective-permute-start | bytes 589832 | tf_op jit(solution)/shard_map/ppermute | solution.py:51
  83.2 12.5 %collective-permute-start.35 = (bf16[128,1152]{1,0:T(8,128)(2,1)S(1)}, bf16[128,1152]{1,0:T(8,128)(2,1)S(1)}, u32[]{:S(2)}, u32[]{:S(2)}) collective-permute-start(bf16[128,1152]{1,0:T(8,128)(2,1)S(1)} %constant_dynamic-update-slice_fusion.44), channel_id=1, source_target_pairs={{0,4},{4,0},{8,12},{12,8},{16,20},{20,16},{24,28},{28,24},{1,5},{5... | collective-permute-start | bytes 884744 | tf_op jit(solution)/shard_map/ppermute | solution.py:19
  91.0 23.3 %collective-permute-start.26 = (bf16[128,1152]{1,0:T(8,128)(2,1)S(1)}, bf16[128,1152]{1,0:T(8,128)(2,1)S(1)}, u32[]{:S(2)}, u32[]{:S(2)}) collective-permute-start(bf16[128,1152]{1,0:T(8,128)(2,1)S(1)} %constant_dynamic-update-slice_fusion.55), channel_id=1, source_target_pairs={{0,8},{4,12},{8,16},{12,20},{16,24},{20,28},{24,0},{28,4},{1,9},{5... | collective-permute-start | bytes 884744 | tf_op jit(solution)/shard_map/ppermute | solution.py:51
  91.0 13.9 %collective-permute-start.36 = (bf16[128,1152]{1,0:T(8,128)(2,1)S(1)}, bf16[128,1152]{1,0:T(8,128)(2,1)S(1)}, u32[]{:S(2)}, u32[]{:S(2)}) collective-permute-start(bf16[128,1152]{1,0:T(8,128)(2,1)S(1)} %constant_dynamic-update-slice_fusion.44), channel_id=1, source_target_pairs={{0,8},{4,12},{8,16},{12,20},{16,24},{20,28},{24,0},{28,4},{1,9},{5... | collective-permute-start | bytes 884744 | tf_op jit(solution)/shard_map/ppermute | solution.py:51
  95.7 10.0 %collective-permute-start.45 = (bf16[128,1152]{1,0:T(8,128)(2,1)S(1)}, bf16[128,1152]{1,0:T(8,128)(2,1)S(1)}, u32[]{:S(2)}, u32[]{:S(2)}) collective-permute-start(bf16[128,1152]{1,0:T(8,128)(2,1)S(1)} %constant_dynamic-update-slice_fusion.33), channel_id=1, source_target_pairs={{0,4},{4,0},{8,12},{12,8},{16,20},{20,16},{24,28},{28,24},{1,5},{5... | collective-permute-start | bytes 884744 | tf_op jit(solution)/shard_map/ppermute | solution.py:19
  114.4 18.1 %collective-permute-start.37 = (bf16[128,1152]{1,0:T(8,128)(2,1)S(1)}, bf16[128,1152]{1,0:T(8,128)(2,1)S(1)}, u32[]{:S(2)}, u32[]{:S(2)}) collective-permute-start(bf16[128,1152]{1,0:T(8,128)(2,1)S(1)} %collective-permute-done.36), channel_id=1, source_target_pairs={{0,4},{4,0},{8,12},{12,8},{16,20},{20,16},{24,28},{28,24},{1,5},{5... | collective-permute-start | bytes 884744 | tf_op jit(solution)/shard_map/ppermute | solution.py:19
  130.3 26.8 %collective-permute-start.56 = (bf16[256,1024]{1,0:T(8,128)(2,1)}, bf16[256,1024]{1,0:T(8,128)(2,1)}, u32[]{:S(2)}, u32[]{:S(2)}) collective-permute-start(bf16[256,1024]{1,0:T(8,128)(2,1)} %bitcast.31), channel_id=1, source_target_pairs={{0,2},{1,3},{2,0},{3,1},{4,6},{5,7},{6,4},{7,5},{8,10},{9,11},{10,... | collective-permute-start | bytes 1572872 | tf_op jit(solution)/shard_map/ppermute | solution.py:19
  132.4 11.2 %collective-permute-start.38 = (bf16[128,1152]{1,0:T(8,128)(2,1)S(1)}, bf16[128,1152]{1,0:T(8,128)(2,1)}, u32[]{:S(2)}, u32[]{:S(2)}) collective-permute-start(bf16[128,1152]{1,0:T(8,128)(2,1)S(1)} %collective-permute-done.36), channel_id=1, source_target_pairs={{0,8},{4,12},{8,16},{12,20},{16,24},{20,28},{24,0},{28,4},{1,9},{5... | collective-permute-start | bytes 884744 | tf_op jit(solution)/shard_map/ppermute | solution.py:51
  132.5 12.9 %collective-permute-start.47 = (bf16[128,1152]{1,0:T(8,128)(2,1)S(1)}, bf16[128,1152]{1,0:T(8,128)(2,1)S(1)}, u32[]{:S(2)}, u32[]{:S(2)}) collective-permute-start(bf16[128,1152]{1,0:T(8,128)(2,1)S(1)} %collective-permute-done.46), channel_id=1, source_target_pairs={{0,4},{4,0},{8,12},{12,8},{16,20},{20,16},{24,28},{28,24},{1,5},{5... | collective-permute-start | bytes 884744 | tf_op jit(solution)/shard_map/ppermute | solution.py:19
  145.4 10.0 %collective-permute-start.28 = (bf16[128,1152]{1,0:T(8,128)(2,1)S(1)}, bf16[128,1152]{1,0:T(8,128)(2,1)}, u32[]{:S(2)}, u32[]{:S(2)}) collective-permute-start(bf16[128,1152]{1,0:T(8,128)(2,1)S(1)} %collective-permute-done.26), channel_id=1, source_target_pairs={{0,8},{4,12},{8,16},{12,20},{16,24},{20,28},{24,0},{28,4},{1,9},{5... | collective-permute-start | bytes 884744 | tf_op jit(solution)/shard_map/ppermute | solution.py:51
  152.3 17.5 %collective-permute-start.2 = (bf16[256,1024]{1,0:T(8,128)(2,1)S(1)}, bf16[256,1024]{1,0:T(8,128)(2,1)S(1)}, u32[]{:S(2)}, u32[]{:S(2)}) collective-permute-start(bf16[256,1024]{1,0:T(8,128)(2,1)S(1)} %collective-permute-done.1), channel_id=1, source_target_pairs={{0,1},{1,0},{2,3},{3,2},{4,5},{5,4},{6,7},{7,6},{8,9},{9,8},{10,11... | collective-permute-start | bytes 1572872 | tf_op jit(solution)/shard_map/ppermute | solution.py:19
  155.4 11.6 %collective-permute-start.39 = (bf16[128,1152]{1,0:T(8,128)(2,1)}, bf16[128,1152]{1,0:T(8,128)(2,1)S(1)}, u32[]{:S(2)}, u32[]{:S(2)}) collective-permute-start(bf16[128,1152]{1,0:T(8,128)(2,1)} %collective-permute-done.38), channel_id=1, source_target_pairs={{0,4},{4,0},{8,12},{12,8},{16,20},{20,16},{24,28},{28,24},{1,5},{5... | collective-permute-start | bytes 884744 | tf_op jit(solution)/shard_map/ppermute | solution.py:19
  157.1 107.2 %collective-permute-start.55 = (bf16[256,1024]{1,0:T(8,128)(2,1)}, bf16[256,1024]{1,0:T(8,128)(2,1)}, u32[]{:S(2)}, u32[]{:S(2)}) collective-permute-start(bf16[256,1024]{1,0:T(8,128)(2,1)} %bitcast.31), channel_id=1, source_target_pairs={{0,1},{1,0},{2,3},{3,2},{4,5},{5,4},{6,7},{7,6},{8,9},{9,8},{10,11... | collective-permute-start | bytes 1572872 | tf_op jit(solution)/shard_map/ppermute | solution.py:19
  161.0 103.3 %collective-permute-start.57 = (bf16[256,1024]{1,0:T(8,128)(2,1)}, bf16[256,1024]{1,0:T(8,128)(2,1)}, u32[]{:S(2)}, u32[]{:S(2)}) collective-permute-start(bf16[256,1024]{1,0:T(8,128)(2,1)} %collective-permute-done.56), channel_id=1, source_target_pairs={{0,1},{1,0},{2,3},{3,2},{4,5},{5,4},{6,7},{7,6},{8,9},{9,8},{10,11... | collective-permute-start | bytes 1572872 | tf_op jit(solution)/shard_map/ppermute | solution.py:19
  167.0 39.4 %collective-permute-start.29 = (bf16[128,1152]{1,0:T(8,128)(2,1)}, bf16[128,1152]{1,0:T(8,128)(2,1)}, u32[]{:S(2)}, u32[]{:S(2)}) collective-permute-start(bf16[128,1152]{1,0:T(8,128)(2,1)} %collective-permute-done.28), channel_id=1, source_target_pairs={{0,4},{4,0},{8,12},{12,8},{16,20},{20,16},{24,28},{28,24},{1,5},{5... | collective-permute-start | bytes 884744 | tf_op jit(solution)/shard_map/ppermute | solution.py:19
  168.0 37.4 %collective-permute-start.49 = (bf16[128,1152]{1,0:T(8,128)(2,1)}, bf16[128,1152]{1,0:T(8,128)(2,1)}, u32[]{:S(2)}, u32[]{:S(2)}) collective-permute-start(bf16[128,1152]{1,0:T(8,128)(2,1)} %collective-permute-done.48), channel_id=1, source_target_pairs={{0,4},{4,0},{8,12},{12,8},{16,20},{20,16},{24,28},{28,24},{1,5},{5... | collective-permute-start | bytes 884744 | tf_op jit(solution)/shard_map/ppermute | solution.py:19
  169.8 33.6 %collective-permute-start.40 = (bf16[128,1152]{1,0:T(8,128)(2,1)}, bf16[128,1152]{1,0:T(8,128)(2,1)}, u32[]{:S(2)}, u32[]{:S(2)}) collective-permute-start(bf16[128,1152]{1,0:T(8,128)(2,1)} %collective-permute-done.38), channel_id=1, source_target_pairs={{0,8},{4,12},{8,16},{12,20},{16,24},{20,28},{24,0},{28,4},{1,9},{5... | collective-permute-start | bytes 884744 | tf_op jit(solution)/shard_map/ppermute | solution.py:51
  203.4 17.1 %collective-permute-start.17 = (bf16[256,1024]{1,0:T(8,128)(2,1)S(1)}, bf16[256,1024]{1,0:T(8,128)(2,1)S(1)}, u32[]{:S(2)}, u32[]{:S(2)}) collective-permute-start(bf16[256,1024]{1,0:T(8,128)(2,1)S(1)} %get-tuple-element.49), channel_id=1, source_target_pairs={{0,1},{1,0},{2,3},{3,2},{4,5},{5,4},{6,7},{7,6},{8,9},{9,8},{10,11... | collective-permute-start | bytes 1572872 | tf_op jit(solution)/shard_map/ppermute | solution.py:19
  205.4 15.3 %collective-permute-start.30 = (bf16[128,1152]{1,0:T(8,128)(2,1)}, bf16[128,1152]{1,0:T(8,128)(2,1)S(1)}, u32[]{:S(2)}, u32[]{:S(2)}) collective-permute-start(bf16[128,1152]{1,0:T(8,128)(2,1)} %collective-permute-done.28), channel_id=1, source_target_pairs={{0,8},{4,12},{8,16},{12,20},{16,24},{20,28},{24,0},{28,4},{1,9},{5... | collective-permute-start | bytes 884744 | tf_op jit(solution)/shard_map/ppermute | solution.py:51
  206.4 23.9 %collective-permute-start.50 = (bf16[128,1152]{1,0:T(8,128)(2,1)}, bf16[128,1152]{1,0:T(8,128)(2,1)S(1)}, u32[]{:S(2)}, u32[]{:S(2)}) collective-permute-start(bf16[128,1152]{1,0:T(8,128)(2,1)} %collective-permute-done.48), channel_id=1, source_target_pairs={{0,8},{4,12},{8,16},{12,20},{16,24},{20,28},{24,0},{28,4},{1,9},{5... | collective-permute-start | bytes 884744 | tf_op jit(solution)/shard_map/ppermute | solution.py:51
  220.5 10.2 %collective-permute-start.16 = (bf16[256,1024]{1,0:T(8,128)(2,1)S(1)}, bf16[256,1024]{1,0:T(8,128)(2,1)S(1)}, u32[]{:S(2)}, u32[]{:S(2)}) collective-permute-start(bf16[256,1024]{1,0:T(8,128)(2,1)S(1)} %get-tuple-element.48), channel_id=1, source_target_pairs={{0,1},{1,0},{2,3},{3,2},{4,5},{5,4},{6,7},{7,6},{8,9},{9,8},{10,11... | collective-permute-start | bytes 1572872 | tf_op jit(solution)/shard_map/ppermute | solution.py:19
  220.8 14.4 %collective-permute-start.18 = (bf16[256,1024]{1,0:T(8,128)(2,1)S(1)}, bf16[256,1024]{1,0:T(8,128)(2,1)S(1)}, u32[]{:S(2)}, u32[]{:S(2)}) collective-permute-start(bf16[256,1024]{1,0:T(8,128)(2,1)S(1)} %add_convert_fusion.5), channel_id=1, source_target_pairs={{0,2},{1,3},{2,0},{3,1},{4,6},{5,7},{6,4},{7,5},{8,10},{9,11},{10,... | collective-permute-start | bytes 1572872 | tf_op jit(solution)/shard_map/ppermute | solution.py:19
  230.3 22.4 %collective-permute-start.31 = (bf16[128,1152]{1,0:T(8,128)(2,1)S(1)}, bf16[128,1152]{1,0:T(8,128)(2,1)S(1)}, u32[]{:S(2)}, u32[]{:S(2)}) collective-permute-start(bf16[128,1152]{1,0:T(8,128)(2,1)S(1)} %collective-permute-done.30), channel_id=1, source_target_pairs={{0,4},{4,0},{8,12},{12,8},{16,20},{20,16},{24,28},{28,24},{1,5},{5... | collective-permute-start | bytes 884744 | tf_op jit(solution)/shard_map/ppermute | solution.py:19
  230.7 22.0 %collective-permute-start.51 = (bf16[128,1152]{1,0:T(8,128)(2,1)S(1)}, bf16[128,1152]{1,0:T(8,128)(2,1)S(1)}, u32[]{:S(2)}, u32[]{:S(2)}) collective-permute-start(bf16[128,1152]{1,0:T(8,128)(2,1)S(1)} %collective-permute-done.50), channel_id=1, source_target_pairs={{0,4},{4,0},{8,12},{12,8},{16,20},{20,16},{24,28},{28,24},{1,5},{5... | collective-permute-start | bytes 884744 | tf_op jit(solution)/shard_map/ppermute | solution.py:19
  235.1 16.5 %collective-permute-start.41 = (bf16[128,1152]{1,0:T(8,128)(2,1)}, bf16[128,1152]{1,0:T(8,128)(2,1)S(1)}, u32[]{:S(2)}, u32[]{:S(2)}) collective-permute-start(bf16[128,1152]{1,0:T(8,128)(2,1)} %collective-permute-done.40), channel_id=1, source_target_pairs={{0,4},{4,0},{8,12},{12,8},{16,20},{20,16},{24,28},{28,24},{1,5},{5... | collective-permute-start | bytes 884744 | tf_op jit(solution)/shard_map/ppermute | solution.py:19
  251.6 12.7 %collective-permute-start.20 = (bf16[256,1024]{1,0:T(8,128)(2,1)S(1)}, bf16[256,1024]{1,0:T(8,128)(2,1)S(1)}, u32[]{:S(2)}, u32[]{:S(2)}) collective-permute-start(bf16[256,1024]{1,0:T(8,128)(2,1)S(1)} %multiply_convert_fusion.2), channel_id=1, source_target_pairs={{0,2},{1,3},{2,0},{3,1},{4,6},{5,7},{6,4},{7,5},{8,10},{9,11},{10,... | collective-permute-start | bytes 1572872 | tf_op jit(solution)/shard_map/ppermute | solution.py:19
  252.8 15.9 %collective-permute-start.19 = (bf16[256,1024]{1,0:T(8,128)(2,1)S(1)}, bf16[256,1024]{1,0:T(8,128)(2,1)S(1)}, u32[]{:S(2)}, u32[]{:S(2)}) collective-permute-start(bf16[256,1024]{1,0:T(8,128)(2,1)S(1)} %multiply_convert_fusion.2), channel_id=1, source_target_pairs={{0,1},{1,0},{2,3},{3,2},{4,5},{5,4},{6,7},{7,6},{8,9},{9,8},{10,11... | collective-permute-start | bytes 1572872 | tf_op jit(solution)/shard_map/ppermute | solution.py:19
  284.7 102.2 %collective-permute-start.52 = (bf16[256,1024]{1,0:T(8,128)(2,1)S(1)}, bf16[256,1024]{1,0:T(8,128)(2,1)S(1)}, u32[]{:S(2)}, u32[]{:S(2)}) collective-permute-start(bf16[256,1024]{1,0:T(8,128)(2,1)S(1)} %get-tuple-element.46), channel_id=1, source_target_pairs={{0,1},{1,0},{2,3},{3,2},{4,5},{5,4},{6,7},{7,6},{8,9},{9,8},{10,11... | collective-permute-start | bytes 1572872 | tf_op jit(solution)/shard_map/ppermute | solution.py:19
  285.3 41.7 %collective-permute-start.53 = (bf16[256,1024]{1,0:T(8,128)(2,1)S(1)}, bf16[256,1024]{1,0:T(8,128)(2,1)S(1)}, u32[]{:S(2)}, u32[]{:S(2)}) collective-permute-start(bf16[256,1024]{1,0:T(8,128)(2,1)S(1)} %get-tuple-element.47), channel_id=1, source_target_pairs={{0,1},{1,0},{2,3},{3,2},{4,5},{5,4},{6,7},{7,6},{8,9},{9,8},{10,11... | collective-permute-start | bytes 1572872 | tf_op jit(solution)/shard_map/ppermute | solution.py:19
  290.0 18.5 %collective-permute-start.100 = (bf16[128,1152]{1,0:T(8,128)(2,1)S(1)}, bf16[128,1152]{1,0:T(8,128)(2,1)S(1)}, u32[]{:S(2)}, u32[]{:S(2)}) collective-permute-start(bf16[128,1152]{1,0:T(8,128)(2,1)S(1)} %get-tuple-element.31), channel_id=1, source_target_pairs={{0,4},{4,0},{8,12},{12,8},{16,20},{20,16},{24,28},{28,24},{1,5},{5... | collective-permute-start | bytes 884744 | tf_op jit(solution)/shard_map/ppermute | solution.py:19
  290.3 38.9 %collective-permute-start.99 = (bf16[128,1152]{1,0:T(8,128)(2,1)S(1)}, bf16[128,1152]{1,0:T(8,128)(2,1)S(1)}, u32[]{:S(2)}, u32[]{:S(2)}) collective-permute-start(bf16[128,1152]{1,0:T(8,128)(2,1)S(1)} %get-tuple-element.32), channel_id=1, source_target_pairs={{0,4},{4,0},{8,12},{12,8},{16,20},{20,16},{24,28},{28,24},{1,5},{5... | collective-permute-start | bytes 884744 | tf_op jit(solution)/shard_map/ppermute | solution.py:19
  292.1 66.3 %collective-permute-start.98 = (bf16[128,1152]{1,0:T(8,128)(2,1)S(1)}, bf16[128,1152]{1,0:T(8,128)(2,1)S(1)}, u32[]{:S(2)}, u32[]{:S(2)}) collective-permute-start(bf16[128,1152]{1,0:T(8,128)(2,1)S(1)} %get-tuple-element.33), channel_id=1, source_target_pairs={{0,4},{4,0},{8,12},{12,8},{16,20},{20,16},{24,28},{28,24},{1,5},{5... | collective-permute-start | bytes 884744 | tf_op jit(solution)/shard_map/ppermute | solution.py:19
  327.0 11.3 %collective-permute-start.101 = (bf16[128,1152]{1,0:T(8,128)(2,1)S(1)}, bf16[128,1152]{1,0:T(8,128)(2,1)S(1)}, u32[]{:S(2)}, u32[]{:S(2)}) collective-permute-start(bf16[128,1152]{1,0:T(8,128)(2,1)S(1)} %add_convert_fusion.9), channel_id=1, source_target_pairs={{0,8},{4,12},{8,16},{12,20},{16,24},{20,28},{24,0},{28,4},{1,9},{5... | collective-permute-start | bytes 884744 | tf_op jit(solution)/shard_map/ppermute | solution.py:51
  328.8 55.5 %collective-permute-start.58 = (bf16[256,1024]{1,0:T(8,128)(2,1)S(1)}, bf16[256,1024]{1,0:T(8,128)(2,1)S(1)}, u32[]{:S(2)}, u32[]{:S(2)}) collective-permute-start(bf16[256,1024]{1,0:T(8,128)(2,1)S(1)} %get-tuple-element.44), channel_id=1, source_target_pairs={{0,1},{1,0},{2,3},{3,2},{4,5},{5,4},{6,7},{7,6},{8,9},{9,8},{10,11... | collective-permute-start | bytes 1572872 | tf_op jit(solution)/shard_map/ppermute | solution.py:19
  338.3 10.4 %collective-permute-start.91 = (bf16[128,1152]{1,0:T(8,128)(2,1)S(1)}, bf16[128,1152]{1,0:T(8,128)(2,1)S(1)}, u32[]{:S(2)}, u32[]{:S(2)}) collective-permute-start(bf16[128,1152]{1,0:T(8,128)(2,1)S(1)} %add_convert_fusion.13), channel_id=1, source_target_pairs={{0,8},{4,12},{8,16},{12,20},{16,24},{20,28},{24,0},{28,4},{1,9},{5... | collective-permute-start | bytes 884744 | tf_op jit(solution)/shard_map/ppermute | solution.py:51
  338.5 10.3 %collective-permute-start.79 = (bf16[128,1152]{1,0:T(8,128)(2,1)S(1)}, bf16[128,1152]{1,0:T(8,128)(2,1)S(1)}, u32[]{:S(2)}, u32[]{:S(2)}) collective-permute-start(bf16[128,1152]{1,0:T(8,128)(2,1)S(1)} %get-tuple-element.40), channel_id=1, source_target_pairs={{0,4},{4,0},{8,12},{12,8},{16,20},{20,16},{24,28},{28,24},{1,5},{5... | collective-permute-start | bytes 884744 | tf_op jit(solution)/shard_map/ppermute | solution.py:19
  348.9 18.2 %collective-permute-start.88 = (bf16[128,1152]{1,0:T(8,128)(2,1)S(1)}, bf16[128,1152]{1,0:T(8,128)(2,1)S(1)}, u32[]{:S(2)}, u32[]{:S(2)}) collective-permute-start(bf16[128,1152]{1,0:T(8,128)(2,1)S(1)} %get-tuple-element.37), channel_id=1, source_target_pairs={{0,4},{4,0},{8,12},{12,8},{16,20},{20,16},{24,28},{28,24},{1,5},{5... | collective-permute-start | bytes 884744 | tf_op jit(solution)/shard_map/ppermute | solution.py:19
  358.4 17.1 %collective-permute-start.78 = (bf16[128,1152]{1,0:T(8,128)(2,1)S(1)}, bf16[128,1152]{1,0:T(8,128)(2,1)S(1)}, u32[]{:S(2)}, u32[]{:S(2)}) collective-permute-start(bf16[128,1152]{1,0:T(8,128)(2,1)S(1)} %get-tuple-element.41), channel_id=1, source_target_pairs={{0,4},{4,0},{8,12},{12,8},{16,20},{20,16},{24,28},{28,24},{1,5},{5... | collective-permute-start | bytes 884744 | tf_op jit(solution)/shard_map/ppermute | solution.py:19
  367.0 17.7 %collective-permute-start.60 = (bf16[256,1024]{1,0:T(8,128)(2,1)S(1)}, bf16[256,1024]{1,0:T(8,128)(2,1)S(1)}, u32[]{:S(2)}, u32[]{:S(2)}) collective-permute-start(bf16[256,1024]{1,0:T(8,128)(2,1)S(1)} %add_convert_fusion.2), channel_id=1, source_target_pairs={{0,2},{1,3},{2,0},{3,1},{4,6},{5,7},{6,4},{7,5},{8,10},{9,11},{10,... | collective-permute-start | bytes 1572872 | tf_op jit(solution)/shard_map/ppermute | solution.py:19
  375.6 21.3 %collective-permute-start.97 = (bf16[128,1152]{1,0:T(8,128)(2,1)S(1)}, bf16[128,1152]{1,0:T(8,128)(2,1)S(1)}, u32[]{:S(2)}, u32[]{:S(2)}) collective-permute-start(bf16[128,1152]{1,0:T(8,128)(2,1)S(1)} %get-tuple-element.30), channel_id=1, source_target_pairs={{0,4},{4,0},{8,12},{12,8},{16,20},{20,16},{24,28},{28,24},{1,5},{5... | collective-permute-start | bytes 884744 | tf_op jit(solution)/shard_map/ppermute | solution.py:19
  383.9 10.4 %collective-permute-start.54 = (bf16[256,1024]{1,0:T(8,128)(2,1)S(1)}, bf16[256,1024]{1,0:T(8,128)(2,1)S(1)}, u32[]{:S(2)}, u32[]{:S(2)}) collective-permute-start(bf16[256,1024]{1,0:T(8,128)(2,1)S(1)} %add_convert_fusion.4), channel_id=1, source_target_pairs={{0,2},{1,3},{2,0},{3,1},{4,6},{5,7},{6,4},{7,5},{8,10},{9,11},{10,... | collective-permute-start | bytes 1572872 | tf_op jit(solution)/shard_map/ppermute | solution.py:19
  384.4 16.3 %collective-permute-start.87 = (bf16[128,1152]{1,0:T(8,128)(2,1)S(1)}, bf16[128,1152]{1,0:T(8,128)(2,1)S(1)}, u32[]{:S(2)}, u32[]{:S(2)}) collective-permute-start(bf16[128,1152]{1,0:T(8,128)(2,1)S(1)} %get-tuple-element.34), channel_id=1, source_target_pairs={{0,4},{4,0},{8,12},{12,8},{16,20},{20,16},{24,28},{28,24},{1,5},{5... | collective-permute-start | bytes 884744 | tf_op jit(solution)/shard_map/ppermute | solution.py:19
  384.7 20.5 %collective-permute-start.77 = (bf16[128,1152]{1,0:T(8,128)(2,1)S(1)}, bf16[128,1152]{1,0:T(8,128)(2,1)S(1)}, u32[]{:S(2)}, u32[]{:S(2)}) collective-permute-start(bf16[128,1152]{1,0:T(8,128)(2,1)S(1)} %get-tuple-element.38), channel_id=1, source_target_pairs={{0,4},{4,0},{8,12},{12,8},{16,20},{20,16},{24,28},{28,24},{1,5},{5... | collective-permute-start | bytes 884744 | tf_op jit(solution)/shard_map/ppermute | solution.py:19
  387.0 11.8 %collective-permute-start.103 = (bf16[128,1152]{1,0:T(8,128)(2,1)S(1)}, bf16[128,1152]{1,0:T(8,128)(2,1)S(1)}, u32[]{:S(2)}, u32[]{:S(2)}) collective-permute-start(bf16[128,1152]{1,0:T(8,128)(2,1)S(1)} %add_convert_fusion.7), channel_id=1, source_target_pairs={{0,8},{4,12},{8,16},{12,20},{16,24},{20,28},{24,0},{28,4},{1,9},{5... | collective-permute-start | bytes 884744 | tf_op jit(solution)/shard_map/ppermute | solution.py:51
  396.8 10.0 %collective-permute-start.83 = (bf16[128,1152]{1,0:T(8,128)(2,1)S(1)}, bf16[128,1152]{1,0:T(8,128)(2,1)S(1)}, u32[]{:S(2)}, u32[]{:S(2)}) collective-permute-start(bf16[128,1152]{1,0:T(8,128)(2,1)S(1)} %add_convert_fusion.15), channel_id=1, source_target_pairs={{0,8},{4,12},{8,16},{12,20},{16,24},{20,28},{24,0},{28,4},{1,9},{5... | collective-permute-start | bytes 884744 | tf_op jit(solution)/shard_map/ppermute | solution.py:51
  398.7 19.9 %collective-permute-start.62 = (bf16[256,1024]{1,0:T(8,128)(2,1)S(1)}, bf16[256,1024]{1,0:T(8,128)(2,1)S(1)}, u32[]{:S(2)}, u32[]{:S(2)}) collective-permute-start(bf16[256,1024]{1,0:T(8,128)(2,1)S(1)} %get-tuple-element.21), channel_id=1, source_target_pairs={{0,2},{1,3},{2,0},{3,1},{4,6},{5,7},{6,4},{7,5},{8,10},{9,11},{10,... | collective-permute-start | bytes 1572872 | tf_op jit(solution)/shard_map/ppermute | solution.py:19
  400.7 21.0 %collective-permute-start.61 = (bf16[256,1024]{1,0:T(8,128)(2,1)S(1)}, bf16[256,1024]{1,0:T(8,128)(2,1)S(1)}, u32[]{:S(2)}, u32[]{:S(2)}) collective-permute-start(bf16[256,1024]{1,0:T(8,128)(2,1)S(1)} %get-tuple-element.21), channel_id=1, source_target_pairs={{0,1},{1,0},{2,3},{3,2},{4,5},{5,4},{6,7},{7,6},{8,9},{9,8},{10,11... | collective-permute-start | bytes 1572872 | tf_op jit(solution)/shard_map/ppermute | solution.py:19
  415.0 58.1 %collective-permute-start.86 = (bf16[32,1152]{1,0:T(8,128)(2,1)S(1)}, bf16[32,1152]{1,0:T(8,128)(2,1)S(1)}, u32[]{:S(2)}, u32[]{:S(2)}) collective-permute-start(bf16[32,1152]{1,0:T(8,128)(2,1)S(1)} %get-tuple-element.71), channel_id=1, source_target_pairs={{0,3},{1,2},{2,1},{3,0},{4,7},{5,6},{6,5},{7,4},{8,11},{9,10},{10,... | collective-permute-start | bytes 221192 | tf_op jit(solution)/shard_map/ppermute | solution.py:19
  473.7 31.1 %collective-permute-start.67 = (bf16[128,768]{0,1:T(8,128)(2,1)}, bf16[128,768]{0,1:T(8,128)(2,1)S(1)}, u32[]{:S(2)}, u32[]{:S(2)}) collective-permute-start(bf16[128,768]{0,1:T(8,128)(2,1)} %get-tuple-element.50), channel_id=1, source_target_pairs={{0,4},{4,0},{8,12},{12,8},{16,20},{20,16},{24,28},{28,24},{1,5},{5... | collective-permute-start | bytes 589832 | tf_op jit(solution)/shard_map/ppermute | solution.py:19
  474.0 18.9 %collective-permute-start.68 = (bf16[128,768]{0,1:T(8,128)(2,1)}, bf16[128,768]{0,1:T(8,128)(2,1)S(1)}, u32[]{:S(2)}, u32[]{:S(2)}) collective-permute-start(bf16[128,768]{0,1:T(8,128)(2,1)} %get-tuple-element.51), channel_id=1, source_target_pairs={{0,4},{4,0},{8,12},{12,8},{16,20},{20,16},{24,28},{28,24},{1,5},{5... | collective-permute-start | bytes 589832 | tf_op jit(solution)/shard_map/ppermute | solution.py:19
  475.8 13.4 %collective-permute-start.69 = (bf16[128,768]{0,1:T(8,128)(2,1)}, bf16[128,768]{0,1:T(8,128)(2,1)}, u32[]{:S(2)}, u32[]{:S(2)}) collective-permute-start(bf16[128,768]{0,1:T(8,128)(2,1)} %get-tuple-element.52), channel_id=1, source_target_pairs={{0,4},{4,0},{8,12},{12,8},{16,20},{20,16},{24,28},{28,24},{1,5},{5... | collective-permute-start | bytes 589832 | tf_op jit(solution)/shard_map/ppermute | solution.py:19
  482.7 44.6 %collective-permute-start.64 = (bf16[256,1024]{1,0:T(8,128)(2,1)}, bf16[256,1024]{1,0:T(8,128)(2,1)}, u32[]{:S(2)}, u32[]{:S(2)}) collective-permute-start(bf16[256,1024]{1,0:T(8,128)(2,1)} %get-tuple-element.42), channel_id=1, source_target_pairs={{0,1},{1,0},{2,3},{3,2},{4,5},{5,4},{6,7},{7,6},{8,9},{9,8},{10,11... | collective-permute-start | bytes 1572872 | tf_op jit(solution)/shard_map/ppermute | solution.py:19
  489.2 12.3 %collective-permute-start.65 = (bf16[256,1024]{1,0:T(8,128)(2,1)}, bf16[256,1024]{1,0:T(8,128)(2,1)}, u32[]{:S(2)}, u32[]{:S(2)}) collective-permute-start(bf16[256,1024]{1,0:T(8,128)(2,1)} %get-tuple-element.43), channel_id=1, source_target_pairs={{0,1},{1,0},{2,3},{3,2},{4,5},{5,4},{6,7},{7,6},{8,9},{9,8},{10,11... | collective-permute-start | bytes 1572872 | tf_op jit(solution)/shard_map/ppermute | solution.py:19
  503.7 23.6 %collective-permute-start.66 = (bf16[256,1024]{1,0:T(8,128)(2,1)}, bf16[256,1024]{1,0:T(8,128)(2,1)}, u32[]{:S(2)}, u32[]{:S(2)}) collective-permute-start(bf16[256,1024]{1,0:T(8,128)(2,1)} %add_convert_fusion.1), channel_id=1, source_target_pairs={{0,2},{1,3},{2,0},{3,1},{4,6},{5,7},{6,4},{7,5},{8,10},{9,11},{10,... | collective-permute-start | bytes 1572872 | tf_op jit(solution)/shard_map/ppermute | solution.py:19
  510.7 10.9 %collective-permute-start.76 = (bf16[32,768]{0,1:T(8,128)(2,1)S(1)}, bf16[32,768]{0,1:T(8,128)(2,1)S(1)}, u32[]{:S(2)}, u32[]{:S(2)}) collective-permute-start(bf16[32,768]{0,1:T(8,128)(2,1)S(1)} %get-tuple-element.102), channel_id=1, source_target_pairs={{0,3},{1,2},{2,1},{3,0},{4,7},{5,6},{6,5},{7,4},{8,11},{9,10},{10,... | collective-permute-start | bytes 147464 | tf_op jit(solution)/shard_map/ppermute | solution.py:19
  510.8 15.1 %collective-permute-start.75 = (bf16[32,768]{0,1:T(8,128)(2,1)S(1)}, bf16[32,768]{0,1:T(8,128)(2,1)S(1)}, u32[]{:S(2)}, u32[]{:S(2)}) collective-permute-start(bf16[32,768]{0,1:T(8,128)(2,1)S(1)} %get-tuple-element.103), channel_id=1, source_target_pairs={{0,2},{1,3},{2,0},{3,1},{4,6},{5,7},{6,4},{7,5},{8,10},{9,11},{10,... | collective-permute-start | bytes 147464 | tf_op jit(solution)/shard_map/ppermute | solution.py:19
  512.0 14.7 %collective-permute-start.74 = (bf16[32,768]{0,1:T(8,128)(2,1)S(1)}, bf16[32,768]{0,1:T(8,128)(2,1)S(1)}, u32[]{:S(2)}, u32[]{:S(2)}) collective-permute-start(bf16[32,768]{0,1:T(8,128)(2,1)S(1)} %get-tuple-element.104), channel_id=1, source_target_pairs={{0,1},{1,0},{2,3},{3,2},{4,5},{5,4},{6,7},{7,6},{8,9},{9,8},{10,11... | collective-permute-start | bytes 147464 | tf_op jit(solution)/shard_map/ppermute | solution.py:19
  (106 other events, 1226.2 us)
where the time goes:
time: 540 us; the launch traced here: 532 us
  waiting for transfers between devices  244 us (45%)
  matrix products  85.8 us (16%)
  starting transfers between devices  66.8 us (12%)
  other arithmetic  47.9 us (9%)
  local copies, waits for them, and re-layouts  42.3 us (8%)
  blocking collectives  41.8 us (8%)
    ppermute x24, waiting for transfers between devices, ring(): return lax.ppermute(value, 'dp', [(i, (i + 2) % size) for i in range(size)])  123 us
    ppermute x88, waiting for transfers between devices, flip(): return lax.ppermute(value, axis, [(i, i ^ bits) for i in range(size)])  121 us
    ppermute x88, starting transfers between devices, flip(): return lax.ppermute(value, axis, [(i, i ^ bits) for i in range(size)])  51.6 us
    all_gather x1, blocking collectives, on_device(): gains_full = lax.all_gather(norm_gains, ALL, axis=1, tiled=True).astype(F32)  41.8 us
    dot_general x7, matrix products, dot(): lax.dot_general(a, b, (((1,), (0,)), ((), ())), preferred_element_type=F32)  20.4 us
    dynamic_update_slice x68, local copies, waits for them, and re-layouts, place(): out = lax.dynamic_update_slice_in_dim(out, part, at * size, axis)  17.8 us
    dot_general x5, matrix products, dot_nt(): lax.dot_general(a, b, (((1,), (1,)), ((), ())), preferred_element_type=F32)  15.9 us
    ppermute x24, starting transfers between devices, ring(): return lax.ppermute(value, 'dp', [(i, (i + 2) % size) for i in range(size)])  15.2 us
  transfers between devices with their start and end apart: 112, of which 50 were waited for; matrix products, arithmetic and copies ran while one was open for 28% of the time, Pallas kernels for 0%

commit v1 on v0

--- a/solution.py
+++ b/solution.py
@@ -9,6 +9,29 @@
 BF = jnp.bfloat16
 F32 = jnp.float32
 ALL = ("dp", "ctx")
+
+
+def laid_out(tiles, dim):
+    dims = list(tiles.shape[1:])
+    dims[dim] *= tiles.shape[0]
+    return jnp.moveaxis(tiles, 0, dim).reshape(dims)
+
+
+def doubled(value, axis):
+    length, index = (lax.axis_size(axis), lax.axis_index(axis))
+    pieces, distance = (value[None], 1)
+    while distance < length:
+        partner_block = lax.ppermute(pieces, axis, [(i, i ^ distance) for i in range(length)])
+        low = index & distance == 0
+        pieces = jnp.concatenate(
+            [jnp.where(low, pieces, partner_block), jnp.where(low, partner_block, pieces)]
+        )
+        distance *= 2
+    return pieces
+
+
+def collect_2(shard, axis, dim):
+    return laid_out(doubled(shard, axis), dim)
 
 
 def add_low(a, b):
@@ -174,7 +197,7 @@
         block = place(exchange_ctx(sent), places, 0)
         return gather_dp(block, dp_size)
 
-    gains_full = lax.all_gather(norm_gains, ALL, axis=1, tiled=True).astype(F32)
+    gains_full = collect_2(norm_gains, ALL, 1).astype(F32)
     attn_w = spread([w_query, key_weight, value_weight, w_output.T])
     wq = attn_w[:, :q_cols]
     wk = attn_w[:, q_cols : q_cols + kv_cols]

time: 540 us -> 515 us (0.954)
  blocking collectives: 41.8 us -> 0 us
  starting transfers between devices: 66.8 us -> 99.8 us
  waiting for transfers between devices: 244 us -> 226 us
    all_gather x1 -> x0, blocking collectives: 41.8 us -> none  [on_device(): gains_full = lax.all_gather(norm_gains, ALL, axis=1, tiled=True).astype(F32)]
    ppermute x88, starting transfers between devices: 51.6 us -> 72.7 us  [flip(): return lax.ppermute(value, axis, [(i, i ^ bits) for i in range(size)])]
    ppermute x24, waiting for transfers between devices: 123 us -> 107 us  [ring(): return lax.ppermute(value, 'dp', [(i, (i + 2) % size) for i in range(size)])]
    ppermute x88, waiting for transfers between devices: 121 us -> 112 us  [flip(): return lax.ppermute(value, axis, [(i, i ^ bits) for i in range(size)])]
    ppermute x0 -> x5, starting transfers between devices: none -> 8.23 us  [doubled(): lax.ppermute(pieces, axis, [(i, i ^ distance) for i in range(length)])]
    ppermute x0 -> x5, waiting for transfers between devices: none -> 7.01 us  [doubled(): lax.ppermute(pieces, axis, [(i, i ^ distance) for i in range(length)])]
  transfers between devices with their start and end apart: 112 -> 117, of which waited for: 50 -> 53; matrix products, arithmetic and copies ran while one was open for 28% -> 29% of each run, Pallas kernels for 0% -> 0%
where the time goes in v1:
time: 515 us; the launch traced here: 507 us
  waiting for transfers between devices  226 us (44%)
  starting transfers between devices  99.8 us (19%)
  matrix products  85.8 us (17%)
  other arithmetic  47.4 us (9%)
  local copies, waits for them, and re-layouts  44.8 us (9%)
    ppermute x88, waiting for transfers between devices, flip(): return lax.ppermute(value, axis, [(i, i ^ bits) for i in range(size)])  112 us
    ppermute x24, waiting for transfers between devices, ring(): return lax.ppermute(value, 'dp', [(i, (i + 2) % size) for i in range(size)])  107 us
    ppermute x88, starting transfers between devices, flip(): return lax.ppermute(value, axis, [(i, i ^ bits) for i in range(size)])  72.7 us
    dot_general x7, matrix products, dot(): lax.dot_general(a, b, (((1,), (0,)), ((), ())), preferred_element_type=F32)  20.3 us
    dynamic_update_slice x68, local copies, waits for them, and re-layouts, place(): out = lax.dynamic_update_slice_in_dim(out, part, at * size, axis)  20.2 us
    ppermute x24, starting transfers between devices, ring(): return lax.ppermute(value, 'dp', [(i, (i + 2) % size) for i in range(size)])  18.9 us
    dot_general x5, matrix products, dot_nt(): lax.dot_general(a, b, (((1,), (1,)), ((), ())), preferred_element_type=F32)  15.9 us
    dot_general x5, matrix products, dot_tn(): lax.dot_general(a, b, (((0,), (0,)), ((), ())), preferred_element_type=F32)  14.5 us
  transfers between devices with their start and end apart: 117, of which 53 were waited for; matrix products, arithmetic and copies ran while one was open for 29% of the time, Pallas kernels for 0%

profile of v1, /device:TPU:0, one launch (start us, length us, event | category | flops | bytes accessed | tf_op | source)
XLA Modules:
  0.0 506.8 jit_solution(18053623180446528727)
XLA Ops:
  1.2 2.6 collective-permute-start.19
  12.6 2.0 collective-permute-start.4
  14.6 3.5 collective-permute-done.4
  19.6 2.1 collective-permute-done.5
  26.5 2.6 collective-permute-start.7
  29.6 2.0 compare_and_fusion
  39.4 3.9 collective-permute-done.38
  43.3 4.2 collective-permute-done.39
  59.3 5.5 %collective-permute-done.11 = bf16[128,768]{1,0:T(8,128)(2,1)S(1)} collective-permute-done((bf16[128,768]{1,0:T(8,128)(2,1)S(1)}, bf16[128,768]{1,0:T(8,128)(2,1)S(1)}, u32[]{:S(2)}, u32[]{:S(2)}) %collective-permute-start.11) | collective-permute-done | bytes 196640 | tf_op jit(solution)/shard_map/ppermute | solution.py:42
  66.5 3.2 collective-permute-done.40
  71.9 7.2 %collective-permute-done.41 = bf16[128,1152]{1,0:T(8,128)(2,1)S(1)} collective-permute-done((bf16[128,1152]{1,0:T(8,128)(2,1)S(1)}, bf16[128,1152]{1,0:T(8,128)(2,1)S(1)}, u32[]{:S(2)}, u32[]{:S(2)}) %collective-permute-start.41) | collective-permute-done | bytes 294944 | tf_op jit(solution)/shard_map/ppermute | solution.py:74
  81.6 6.2 %collective-permute-done.51 = bf16[128,1152]{1,0:T(8,128)(2,1)S(1)} collective-permute-done((bf16[128,1152]{1,0:T(8,128)(2,1)S(1)}, bf16[128,1152]{1,0:T(8,128)(2,1)S(1)}, u32[]{:S(2)}, u32[]{:S(2)}) %collective-permute-start.51) | collective-permute-done | bytes 294944 | tf_op jit(solution)/shard_map/ppermute | solution.py:74
  90.2 6.6 %collective-permute-done.14 = bf16[128,768]{1,0:T(8,128)(2,1)S(1)} collective-permute-done((bf16[128,768]{1,0:T(8,128)(2,1)S(1)}, bf16[128,768]{1,0:T(8,128)(2,1)S(1)}, u32[]{:S(2)}, u32[]{:S(2)}) %collective-permute-start.14) | collective-permute-done | bytes 196640 | tf_op jit(solution)/shard_map/ppermute | solution.py:74
  98.4 6.2 %collective-permute-done.15 = bf16[128,768]{1,0:T(8,128)(2,1)S(1)} collective-permute-done((bf16[128,768]{1,0:T(8,128)(2,1)S(1)}, bf16[128,768]{1,0:T(8,128)(2,1)S(1)}, u32[]{:S(2)}, u32[]{:S(2)}) %collective-permute-start.15) | collective-permute-done | bytes 196640 | tf_op jit(solution)/shard_map/ppermute | solution.py:42
  108.7 9.4 %collective-permute-done.43 = bf16[128,1152]{1,0:T(8,128)(2,1)} collective-permute-done((bf16[128,1152]{1,0:T(8,128)(2,1)S(1)}, bf16[128,1152]{1,0:T(8,128)(2,1)}, u32[]{:S(2)}, u32[]{:S(2)}) %collective-permute-start.43) | collective-permute-done | bytes 294944 | tf_op jit(solution)/shard_map/ppermute | solution.py:74
  121.5 5.3 %collective-permute-done.53 = bf16[128,1152]{1,0:T(8,128)(2,1)} collective-permute-done((bf16[128,1152]{1,0:T(8,128)(2,1)S(1)}, bf16[128,1152]{1,0:T(8,128)(2,1)}, u32[]{:S(2)}, u32[]{:S(2)}) %collective-permute-start.53) | collective-permute-done | bytes 294944 | tf_op jit(solution)/shard_map/ppermute | solution.py:74
  132.5 3.0 collective-permute-done.17
  135.6 5.9 %collective-permute-done.44 = bf16[128,1152]{1,0:T(8,128)(2,1)S(1)} collective-permute-done((bf16[128,1152]{1,0:T(8,128)(2,1)}, bf16[128,1152]{1,0:T(8,128)(2,1)S(1)}, u32[]{:S(2)}, u32[]{:S(2)}) %collective-permute-start.44) | collective-permute-done | bytes 294944 | tf_op jit(solution)/shard_map/ppermute | solution.py:42
  144.8 4.8 fusion.15
  153.9 7.4 %fusion.96 = (f32[2,2,1024]{2,1,0:T(2,128)S(1)}, f32[2,2,1024,1024]{2,3,1,0:T(8,128)}) fusion(bf16[1024,2,64,1]{0,2,3,1:T(8,128)(2,1)S(1)} %fusion.47, bf16[1024,2,2,64]{0,3,2,1:T(8,128)(2,1)S(1)} %fusion.34, pred[1024,1024]{0,1:T(8,128)(4,1)S(1)} %copy-done.26), kind=kOutput, calls=%fused_computation.362 | convolution fusion | flops 549449728 | bytes 18628608 | tf_op jit(solution)/shard_map/tkgd,skd->kgts/dot_general | solution.py:231
  161.4 8.0 %fusion.3 = f32[2,2,1024]{2,1,0:T(2,128)S(1)} fusion(f32[2,2,1024,1024]{2,3,1,0:T(8,128)} %get-tuple-element.148, f32[2,2,1024]{2,1,0:T(2,128)S(1)} %get-tuple-element.147), kind=kLoop, calls=%fused_computation.9 | loop fusion | flops 8384512 | bytes 16809984 | tf_op jit(solution)/shard_map/reduce_sum | solution.py:237
  169.4 7.5 %fusion.18 = bf16[2,64,2,1024]{3,1,2,0:T(8,128)(2,1)S(1)} fusion(bf16[1024,2,64,1]{0,2,3,1:T(8,128)(2,1)S(1)} %bitcast.149, f32[2,2,1024,1024]{2,3,1,0:T(8,128)} %get-tuple-element.148, f32[2,2,1024]{2,1,0:T(2,128)S(1)} %fusion.3, f32[2,2,1024]{2,1,0:T(2,128)S(1)} %get-tuple-element.147), kind=kOutput, calls=%fused_computation.68 | convolution fusion | flops 549715968 | bytes 17596416 | tf_op jit(solution)/shard_map/kgts,skd->tkgd/dot_general | solution.py:240
  180.9 13.0 %collective-permute-start.55 = (bf16[128,1152]{1,0:T(8,128)(2,1)}, bf16[128,1152]{1,0:T(8,128)(2,1)S(1)}, u32[]{:S(2)}, u32[]{:S(2)}) collective-permute-start(bf16[128,1152]{1,0:T(8,128)(2,1)} %collective-permute-done.53), channel_id=1, source_target_pairs={{0,8},{4,12},{8,16},{12,20},{16,24},{20,28},{24,0},{28,4},{1,9},{5... | collective-permute-start | bytes 884744 | tf_op jit(solution)/shard_map/ppermute | solution.py:74
  196.3 8.4 %collective-permute-done.55 = bf16[128,1152]{1,0:T(8,128)(2,1)S(1)} collective-permute-done((bf16[128,1152]{1,0:T(8,128)(2,1)}, bf16[128,1152]{1,0:T(8,128)(2,1)S(1)}, u32[]{:S(2)}, u32[]{:S(2)}) %collective-permute-start.55) | collective-permute-done | bytes 294944 | tf_op jit(solution)/shard_map/ppermute | solution.py:74
  206.9 2.7 collective-permute-done.23
  211.7 14.4 %collective-permute-done.46 = bf16[128,1152]{1,0:T(8,128)(2,1)S(1)} collective-permute-done((bf16[128,1152]{1,0:T(8,128)(2,1)}, bf16[128,1152]{1,0:T(8,128)(2,1)S(1)}, u32[]{:S(2)}, u32[]{:S(2)}) %collective-permute-start.46) | collective-permute-done | bytes 294944 | tf_op jit(solution)/shard_map/ppermute | solution.py:42
  228.0 10.7 %collective-permute-done.25 = bf16[256,1024]{1,0:T(8,128)(2,1)S(1)} collective-permute-done((bf16[256,1024]{1,0:T(8,128)(2,1)S(1)}, bf16[256,1024]{1,0:T(8,128)(2,1)S(1)}, u32[]{:S(2)}, u32[]{:S(2)}) %collective-permute-start.25) | collective-permute-done | bytes 524320 | tf_op jit(solution)/shard_map/ppermute | solution.py:42
  238.7 4.4 fusion.46
  243.1 4.5 fusion.77
  247.7 8.2 %fusion.13 = (bf16[1024,1152]{1,0:T(8,128)(2,1)}, bf16[1024,1152]{1,0:T(8,128)(2,1)}, bf16[1024,1152]{1,0:T(8,128)(2,1)S(1)}) fusion(f32[1024,1152]{1,0:T(8,128)S(1)} %fusion.46, f32[1024,1152]{1,0:T(8,128)S(1)} %fusion.77, bf16[1024,1152]{1,0:T(8,128)(2,1)S(1)} %constant_dynamic-update-slice_fusion.47, bf16[256,1024]{1,0:T(8,128)(2,1)S(1)} %collective-permute-done.26, ...), kind=kOutput, calls=%fused_computation.21 | convolution fusion | flops 2443182080 | bytes 20971520 | tf_op jit(solution)/shard_map/dot_general | solution.py:122
  255.9 3.1 convolution_convert_fusion.3
  259.7 4.4 convolution_convert_fusion
  268.0 4.6 fusion.97
  272.5 3.2 convolution_convert_fusion.1
  277.4 3.1 add_convert_fusion
  280.6 3.4 convolution_convert_fusion.2
  284.8 8.0 %collective-permute-done.95 = bf16[128,1152]{1,0:T(8,128)(2,1)S(1)} collective-permute-done((bf16[128,1152]{1,0:T(8,128)(2,1)S(1)}, bf16[128,1152]{1,0:T(8,128)(2,1)S(1)}, u32[]{:S(2)}, u32[]{:S(2)}) %collective-permute-start.95) | collective-permute-done | bytes 294944 | tf_op jit(solution)/shard_map/ppermute | solution.py:42
  294.4 6.8 %collective-permute-done.85 = bf16[128,1152]{1,0:T(8,128)(2,1)S(1)} collective-permute-done((bf16[128,1152]{1,0:T(8,128)(2,1)S(1)}, bf16[128,1152]{1,0:T(8,128)(2,1)S(1)}, u32[]{:S(2)}, u32[]{:S(2)}) %collective-permute-start.85) | collective-permute-done | bytes 294944 | tf_op jit(solution)/shard_map/ppermute | solution.py:42
  305.2 7.3 %collective-permute-done.106 = bf16[128,1152]{1,0:T(8,128)(2,1)S(1)} collective-permute-done((bf16[128,1152]{1,0:T(8,128)(2,1)S(1)}, bf16[128,1152]{1,0:T(8,128)(2,1)S(1)}, u32[]{:S(2)}, u32[]{:S(2)}) %collective-permute-start.106) | collective-permute-done | bytes 294944 | tf_op jit(solution)/shard_map/ppermute | solution.py:74
  314.5 8.4 %collective-permute-done.96 = bf16[128,1152]{1,0:T(8,128)(2,1)S(1)} collective-permute-done((bf16[128,1152]{1,0:T(8,128)(2,1)S(1)}, bf16[128,1152]{1,0:T(8,128)(2,1)S(1)}, u32[]{:S(2)}, u32[]{:S(2)}) %collective-permute-start.96) | collective-permute-done | bytes 294944 | tf_op jit(solution)/shard_map/ppermute | solution.py:74
  324.9 7.6 %collective-permute-done.86 = bf16[128,1152]{1,0:T(8,128)(2,1)S(1)} collective-permute-done((bf16[128,1152]{1,0:T(8,128)(2,1)S(1)}, bf16[128,1152]{1,0:T(8,128)(2,1)S(1)}, u32[]{:S(2)}, u32[]{:S(2)}) %collective-permute-start.86) | collective-permute-done | bytes 294944 | tf_op jit(solution)/shard_map/ppermute | solution.py:74
  334.4 6.7 %collective-permute-done.107 = bf16[128,1152]{1,0:T(8,128)(2,1)S(1)} collective-permute-done((bf16[128,1152]{1,0:T(8,128)(2,1)S(1)}, bf16[128,1152]{1,0:T(8,128)(2,1)S(1)}, u32[]{:S(2)}, u32[]{:S(2)}) %collective-permute-start.107) | collective-permute-done | bytes 294944 | tf_op jit(solution)/shard_map/ppermute | solution.py:74
  342.3 7.3 %collective-permute-done.97 = bf16[128,1152]{1,0:T(8,128)(2,1)S(1)} collective-permute-done((bf16[128,1152]{1,0:T(8,128)(2,1)S(1)}, bf16[128,1152]{1,0:T(8,128)(2,1)S(1)}, u32[]{:S(2)}, u32[]{:S(2)}) %collective-permute-start.97) | collective-permute-done | bytes 294944 | tf_op jit(solution)/shard_map/ppermute | solution.py:74
  351.5 6.6 %collective-permute-done.87 = bf16[128,1152]{1,0:T(8,128)(2,1)S(1)} collective-permute-done((bf16[128,1152]{1,0:T(8,128)(2,1)S(1)}, bf16[128,1152]{1,0:T(8,128)(2,1)S(1)}, u32[]{:S(2)}, u32[]{:S(2)}) %collective-permute-start.87) | collective-permute-done | bytes 294944 | tf_op jit(solution)/shard_map/ppermute | solution.py:74
  361.9 6.6 %collective-permute-done.59 = bf16[256,1024]{1,0:T(8,128)(2,1)S(1)} collective-permute-done((bf16[256,1024]{1,0:T(8,128)(2,1)S(1)}, bf16[256,1024]{1,0:T(8,128)(2,1)S(1)}, u32[]{:S(2)}, u32[]{:S(2)}) %collective-permute-start.59) | collective-permute-done | bytes 524320 | tf_op jit(solution)/shard_map/ppermute | solution.py:42
  368.5 2.5 fusion.80
  371.0 2.6 collective-permute-done.108
  375.0 2.9 collective-permute-done.98
  383.7 2.4 collective-permute-done.110
  398.0 3.9 fusion.22
  401.9 8.5 %fusion = (f32[2,2,1024]{2,1,0:T(2,128)S(1)}, f32[2,1024,1024,2]{2,1,3,0:T(8,128)}) fusion(f32[2,2,1024,1024]{2,3,1,0:T(8,128)S(1)} %bitcast.136, f32[2,2,1024]{2,1,0:T(2,128)S(1)} %log_add_fusion, bf16[1024,2,64,1]{0,2,3,1:T(8,128)(2,1)} %bitcast.150, bf16[1024,2,2,64]{0,3,2,1:T(8,128)(2,1)S(1)} %bitcast.146), kind=kOutput, calls=%fused_computation.2 | convolution fusion | flops 549449728 | bytes 34373632 | tf_op jit(solution)/shard_map/tkgd,skd->kgts/dot_general | solution.py:280
  410.4 8.3 %fusion.2 = bf16[2,2,1024,1024]{2,3,1,0:T(8,128)(2,1)S(1)} fusion(f32[2,1024,1024,2]{2,1,3,0:T(8,128)} %get-tuple-element.150, f32[2,2,1024,1024]{2,3,1,0:T(8,128)S(1)} %bitcast.136, f32[2,2,1024]{2,1,0:T(2,128)S(1)} %get-tuple-element.149, f32[2,2,1024]{2,1,0:T(2,128)S(1)} %log_add_fusion), kind=kLoop, calls=%fused_computation.4 | loop fusion | flops 16777216 | bytes 41975808 | tf_op jit(solution)/shard_map/convert_element_type | solution.py:285
  422.1 6.1 %broadcast_multiply_fusion = (f32[1024,2,64]{0,2,1:T(8,128)S(1)}, f32[1024,2,64]{0,2,1:T(8,128)S(1)}) fusion(f32[1024,64]{0,1:T(8,128)S(1)} %copy-done.16, bf16[1024,2,2,64]{0,3,2,1:T(8,128)(2,1)S(1)} %copy-done.18, bf16[2,2,1024,1024]{2,3,1,0:T(8,128)(2,1)} %copy-done), kind=kOutput, calls=%fused_computation.148 | convolution fusion | flops 537001984 | bytes 10223616 | tf_op jit(solution)/shard_map/kgts,tkgd->skd/dot_general | solution.py:290
  432.3 4.3 fusion.16
  436.9 2.2 convolution_convert_fusion.6
  451.2 3.3 collective-permute-start.116
  455.3 2.0 collective-permute-start.76
  459.0 5.1 %collective-permute-done.74 = bf16[128,768]{0,1:T(8,128)(2,1)} collective-permute-done((bf16[128,768]{0,1:T(8,128)(2,1)}, bf16[128,768]{0,1:T(8,128)(2,1)}, u32[]{:S(2)}, u32[]{:S(2)}) %collective-permute-start.74) | collective-permute-done | bytes 196640 | tf_op jit(solution)/shard_map/ppermute | solution.py:42
  467.7 7.6 %collective-permute-done.77 = bf16[128,768]{0,1:T(8,128)(2,1)} collective-permute-done((bf16[128,768]{0,1:T(8,128)(2,1)}, bf16[128,768]{0,1:T(8,128)(2,1)}, u32[]{:S(2)}, u32[]{:S(2)}) %collective-permute-start.77) | collective-permute-done | bytes 196640 | tf_op jit(solution)/shard_map/ppermute | solution.py:74
  476.4 2.2 add_convert_fusion.1
  479.7 5.0 collective-permute-done.78
  487.6 8.8 %collective-permute-done.81 = bf16[32,768]{0,1:T(8,128)(2,1)S(1)} collective-permute-done((bf16[32,768]{0,1:T(8,128)(2,1)S(1)}, bf16[32,768]{0,1:T(8,128)(2,1)S(1)}, u32[]{:S(2)}, u32[]{:S(2)}) %collective-permute-start.81) | collective-permute-done | bytes 49184 | tf_op jit(solution)/shard_map/ppermute | solution.py:42
  496.5 4.3 collective-permute-done.80
  504.0 2.6 fusion.39
  (533 shorter events, 157.0 us)
Async XLA Ops:
  0.7 24.8 %collective-permute-start.18 = (s32[1,256]{1,0:T(1,128)}, s32[1,256]{1,0:T(1,128)S(1)}, u32[]{:S(2)}, u32[]{:S(2)}) collective-permute-start(s32[1,256]{1,0:T(1,128)} %param.13), channel_id=1, source_target_pairs={{0,1},{1,0},{2,3},{3,2},{4,5},{5,4},{6,7},{7,6},{8,9},{9,8},{10,11... | collective-permute-start | bytes 3080 | tf_op jit(solution)/shard_map/ppermute | solution.py:42
  1.2 22.2 %collective-permute-start.19 = (s32[1,256]{1,0:T(1,128)}, s32[1,256]{1,0:T(1,128)S(1)}, u32[]{:S(2)}, u32[]{:S(2)}) collective-permute-start(s32[1,256]{1,0:T(1,128)} %param.13), channel_id=1, source_target_pairs={{0,2},{1,3},{2,0},{3,1},{4,6},{5,7},{6,4},{7,5},{8,10},{9,11},{10,... | collective-permute-start | bytes 3080 | tf_op jit(solution)/shard_map/ppermute | solution.py:42
  3.8 117.6 %collective-permute-start.1 = (bf16[256,1024]{1,0:T(8,128)(2,1)}, bf16[256,1024]{1,0:T(8,128)(2,1)S(1)}, u32[]{:S(2)}, u32[]{:S(2)}) collective-permute-start(bf16[256,1024]{1,0:T(8,128)(2,1)} %bitcast.140), channel_id=1, source_target_pairs={{0,2},{1,3},{2,0},{3,1},{4,6},{5,7},{6,4},{7,5},{8,10},{9,11},{10,... | collective-permute-start | bytes 1572872 | tf_op jit(solution)/shard_map/ppermute | solution.py:42
  3.8 139.9 %collective-permute-start = (bf16[256,1024]{1,0:T(8,128)(2,1)}, bf16[256,1024]{1,0:T(8,128)(2,1)S(1)}, u32[]{:S(2)}, u32[]{:S(2)}) collective-permute-start(bf16[256,1024]{1,0:T(8,128)(2,1)} %bitcast.141), channel_id=1, source_target_pairs={{0,1},{1,0},{2,3},{3,2},{4,5},{5,4},{6,7},{7,6},{8,9},{9,8},{10,11... | collective-permute-start | bytes 1572872 | tf_op jit(solution)/shard_map/ppermute | solution.py:42
  23.4 13.0 %collective-permute-start.9 = (bf16[32,768]{1,0:T(8,128)(2,1)}, bf16[32,768]{1,0:T(8,128)(2,1)}, u32[]{:S(2)}, u32[]{:S(2)}) collective-permute-start(bf16[32,768]{1,0:T(8,128)(2,1)} %pad_maximum_fusion.13), channel_id=1, source_target_pairs={{0,2},{1,3},{2,0},{3,1},{4,6},{5,7},{6,4},{7,5},{8,10},{9,11},{10,... | collective-permute-start | bytes 147464 | tf_op jit(solution)/shard_map/ppermute | solution.py:42
  33.9 18.2 %collective-permute-start.49 = (bf16[32,1152]{1,0:T(8,128)(2,1)S(1)}, bf16[32,1152]{1,0:T(8,128)(2,1)S(1)}, u32[]{:S(2)}, u32[]{:S(2)}) collective-permute-start(bf16[32,1152]{1,0:T(8,128)(2,1)S(1)} %get-tuple-element.77), channel_id=1, source_target_pairs={{0,3},{1,2},{2,1},{3,0},{4,7},{5,6},{6,5},{7,4},{8,11},{9,10},{10,... | collective-permute-start | bytes 221192 | tf_op jit(solution)/shard_map/ppermute | solution.py:42
  36.4 14.4 %collective-permute-start.47 = (bf16[32,1152]{1,0:T(8,128)(2,1)S(1)}, bf16[32,1152]{1,0:T(8,128)(2,1)S(1)}, u32[]{:S(2)}, u32[]{:S(2)}) collective-permute-start(bf16[32,1152]{1,0:T(8,128)(2,1)S(1)} %get-tuple-element.78), channel_id=1, source_target_pairs={{0,1},{1,0},{2,3},{3,2},{4,5},{5,4},{6,7},{7,6},{8,9},{9,8},{10,11... | collective-permute-start | bytes 221192 | tf_op jit(solution)/shard_map/ppermute | solution.py:42
  53.3 13.0 %collective-permute-start.12 = (bf16[128,768]{1,0:T(8,128)(2,1)S(1)}, bf16[128,768]{1,0:T(8,128)(2,1)S(1)}, u32[]{:S(2)}, u32[]{:S(2)}) collective-permute-start(bf16[128,768]{1,0:T(8,128)(2,1)S(1)} %constant_dynamic-update-slice_fusion.66), channel_id=1, source_target_pairs={{0,8},{4,12},{8,16},{12,20},{16,24},{20,28},{24,0},{28,4},{1,9},{5... | collective-permute-start | bytes 589832 | tf_op jit(solution)/shard_map/ppermute | solution.py:74
  58.4 11.2 %collective-permute-start.40 = (bf16[128,1152]{1,0:T(8,128)(2,1)S(1)}, bf16[128,1152]{1,0:T(8,128)(2,1)S(1)}, u32[]{:S(2)}, u32[]{:S(2)}) collective-permute-start(bf16[128,1152]{1,0:T(8,128)(2,1)S(1)} %constant_dynamic-update-slice_fusion.44), channel_id=1, source_target_pairs={{0,4},{4,0},{8,12},{12,8},{16,20},{20,16},{24,28},{28,24},{1,5},{5... | collective-permute-start | bytes 884744 | tf_op jit(solution)/shard_map/ppermute | solution.py:42
  64.7 24.8 %collective-permute-start.31 = (bf16[128,1152]{1,0:T(8,128)(2,1)S(1)}, bf16[128,1152]{1,0:T(8,128)(2,1)S(1)}, u32[]{:S(2)}, u32[]{:S(2)}) collective-permute-start(bf16[128,1152]{1,0:T(8,128)(2,1)S(1)} %constant_dynamic-update-slice_fusion.55), channel_id=1, source_target_pairs={{0,8},{4,12},{8,16},{12,20},{16,24},{20,28},{24,0},{28,4},{1,9},{5... | collective-permute-start | bytes 884744 | tf_op jit(solution)/shard_map/ppermute | solution.py:74
  66.4 12.7 %collective-permute-start.41 = (bf16[128,1152]{1,0:T(8,128)(2,1)S(1)}, bf16[128,1152]{1,0:T(8,128)(2,1)S(1)}, u32[]{:S(2)}, u32[]{:S(2)}) collective-permute-start(bf16[128,1152]{1,0:T(8,128)(2,1)S(1)} %constant_dynamic-update-slice_fusion.44), channel_id=1, source_target_pairs={{0,8},{4,12},{8,16},{12,20},{16,24},{20,28},{24,0},{28,4},{1,9},{5... | collective-permute-start | bytes 884744 | tf_op jit(solution)/shard_map/ppermute | solution.py:74
  69.7 10.5 %collective-permute-start.50 = (bf16[128,1152]{1,0:T(8,128)(2,1)S(1)}, bf16[128,1152]{1,0:T(8,128)(2,1)S(1)}, u32[]{:S(2)}, u32[]{:S(2)}) collective-permute-start(bf16[128,1152]{1,0:T(8,128)(2,1)S(1)} %constant_dynamic-update-slice_fusion.33), channel_id=1, source_target_pairs={{0,4},{4,0},{8,12},{12,8},{16,20},{20,16},{24,28},{28,24},{1,5},{5... | collective-permute-start | bytes 884744 | tf_op jit(solution)/shard_map/ppermute | solution.py:42
  89.6 16.8 %collective-permute-start.42 = (bf16[128,1152]{1,0:T(8,128)(2,1)S(1)}, bf16[128,1152]{1,0:T(8,128)(2,1)S(1)}, u32[]{:S(2)}, u32[]{:S(2)}) collective-permute-start(bf16[128,1152]{1,0:T(8,128)(2,1)S(1)} %collective-permute-done.41), channel_id=1, source_target_pairs={{0,4},{4,0},{8,12},{12,8},{16,20},{20,16},{24,28},{28,24},{1,5},{5... | collective-permute-start | bytes 884744 | tf_op jit(solution)/shard_map/ppermute | solution.py:42
  104.6 27.8 %collective-permute-start.61 = (bf16[256,1024]{1,0:T(8,128)(2,1)}, bf16[256,1024]{1,0:T(8,128)(2,1)}, u32[]{:S(2)}, u32[]{:S(2)}) collective-permute-start(bf16[256,1024]{1,0:T(8,128)(2,1)} %bitcast.28), channel_id=1, source_target_pairs={{0,2},{1,3},{2,0},{3,1},{4,6},{5,7},{6,4},{7,5},{8,10},{9,11},{10,... | collective-permute-start | bytes 1572872 | tf_op jit(solution)/shard_map/ppermute | solution.py:42
  106.3 11.8 %collective-permute-start.43 = (bf16[128,1152]{1,0:T(8,128)(2,1)S(1)}, bf16[128,1152]{1,0:T(8,128)(2,1)}, u32[]{:S(2)}, u32[]{:S(2)}) collective-permute-start(bf16[128,1152]{1,0:T(8,128)(2,1)S(1)} %collective-permute-done.41), channel_id=1, source_target_pairs={{0,8},{4,12},{8,16},{12,20},{16,24},{20,28},{24,0},{28,4},{1,9},{5... | collective-permute-start | bytes 884744 | tf_op jit(solution)/shard_map/ppermute | solution.py:74
  106.4 13.5 %collective-permute-start.52 = (bf16[128,1152]{1,0:T(8,128)(2,1)S(1)}, bf16[128,1152]{1,0:T(8,128)(2,1)S(1)}, u32[]{:S(2)}, u32[]{:S(2)}) collective-permute-start(bf16[128,1152]{1,0:T(8,128)(2,1)S(1)} %collective-permute-done.51), channel_id=1, source_target_pairs={{0,4},{4,0},{8,12},{12,8},{16,20},{20,16},{24,28},{28,24},{1,5},{5... | collective-permute-start | bytes 884744 | tf_op jit(solution)/shard_map/ppermute | solution.py:42
  126.7 17.5 %collective-permute-start.2 = (bf16[256,1024]{1,0:T(8,128)(2,1)S(1)}, bf16[256,1024]{1,0:T(8,128)(2,1)S(1)}, u32[]{:S(2)}, u32[]{:S(2)}) collective-permute-start(bf16[256,1024]{1,0:T(8,128)(2,1)S(1)} %collective-permute-done.1), channel_id=1, source_target_pairs={{0,1},{1,0},{2,3},{3,2},{4,5},{5,4},{6,7},{7,6},{8,9},{9,8},{10,11... | collective-permute-start | bytes 1572872 | tf_op jit(solution)/shard_map/ppermute | solution.py:42
  130.1 11.4 %collective-permute-start.44 = (bf16[128,1152]{1,0:T(8,128)(2,1)}, bf16[128,1152]{1,0:T(8,128)(2,1)S(1)}, u32[]{:S(2)}, u32[]{:S(2)}) collective-permute-start(bf16[128,1152]{1,0:T(8,128)(2,1)} %collective-permute-done.43), channel_id=1, source_target_pairs={{0,4},{4,0},{8,12},{12,8},{16,20},{20,16},{24,28},{28,24},{1,5},{5... | collective-permute-start | bytes 884744 | tf_op jit(solution)/shard_map/ppermute | solution.py:42
  132.4 106.3 %collective-permute-start.60 = (bf16[256,1024]{1,0:T(8,128)(2,1)}, bf16[256,1024]{1,0:T(8,128)(2,1)}, u32[]{:S(2)}, u32[]{:S(2)}) collective-permute-start(bf16[256,1024]{1,0:T(8,128)(2,1)} %bitcast.28), channel_id=1, source_target_pairs={{0,1},{1,0},{2,3},{3,2},{4,5},{5,4},{6,7},{7,6},{8,9},{9,8},{10,11... | collective-permute-start | bytes 1572872 | tf_op jit(solution)/shard_map/ppermute | solution.py:42
  135.5 103.2 %collective-permute-start.62 = (bf16[256,1024]{1,0:T(8,128)(2,1)}, bf16[256,1024]{1,0:T(8,128)(2,1)}, u32[]{:S(2)}, u32[]{:S(2)}) collective-permute-start(bf16[256,1024]{1,0:T(8,128)(2,1)} %collective-permute-done.61), channel_id=1, source_target_pairs={{0,1},{1,0},{2,3},{3,2},{4,5},{5,4},{6,7},{7,6},{8,9},{9,8},{10,11... | collective-permute-start | bytes 1572872 | tf_op jit(solution)/shard_map/ppermute | solution.py:42
  141.4 39.5 %collective-permute-start.34 = (bf16[128,1152]{1,0:T(8,128)(2,1)}, bf16[128,1152]{1,0:T(8,128)(2,1)}, u32[]{:S(2)}, u32[]{:S(2)}) collective-permute-start(bf16[128,1152]{1,0:T(8,128)(2,1)} %collective-permute-done.33), channel_id=1, source_target_pairs={{0,4},{4,0},{8,12},{12,8},{16,20},{20,16},{24,28},{28,24},{1,5},{5... | collective-permute-start | bytes 884744 | tf_op jit(solution)/shard_map/ppermute | solution.py:42
  143.7 36.2 %collective-permute-start.54 = (bf16[128,1152]{1,0:T(8,128)(2,1)}, bf16[128,1152]{1,0:T(8,128)(2,1)}, u32[]{:S(2)}, u32[]{:S(2)}) collective-permute-start(bf16[128,1152]{1,0:T(8,128)(2,1)} %collective-permute-done.53), channel_id=1, source_target_pairs={{0,4},{4,0},{8,12},{12,8},{16,20},{20,16},{24,28},{28,24},{1,5},{5... | collective-permute-start | bytes 884744 | tf_op jit(solution)/shard_map/ppermute | solution.py:42
  144.2 33.6 %collective-permute-start.45 = (bf16[128,1152]{1,0:T(8,128)(2,1)}, bf16[128,1152]{1,0:T(8,128)(2,1)}, u32[]{:S(2)}, u32[]{:S(2)}) collective-permute-start(bf16[128,1152]{1,0:T(8,128)(2,1)} %collective-permute-done.43), channel_id=1, source_target_pairs={{0,8},{4,12},{8,16},{12,20},{16,24},{20,28},{24,0},{28,4},{1,9},{5... | collective-permute-start | bytes 884744 | tf_op jit(solution)/shard_map/ppermute | solution.py:74
  177.9 17.1 %collective-permute-start.22 = (bf16[256,1024]{1,0:T(8,128)(2,1)S(1)}, bf16[256,1024]{1,0:T(8,128)(2,1)S(1)}, u32[]{:S(2)}, u32[]{:S(2)}) collective-permute-start(bf16[256,1024]{1,0:T(8,128)(2,1)S(1)} %get-tuple-element.51), channel_id=1, source_target_pairs={{0,1},{1,0},{2,3},{3,2},{4,5},{5,4},{6,7},{7,6},{8,9},{9,8},{10,11... | collective-permute-start | bytes 1572872 | tf_op jit(solution)/shard_map/ppermute | solution.py:42
  179.9 15.3 %collective-permute-start.35 = (bf16[128,1152]{1,0:T(8,128)(2,1)}, bf16[128,1152]{1,0:T(8,128)(2,1)S(1)}, u32[]{:S(2)}, u32[]{:S(2)}) collective-permute-start(bf16[128,1152]{1,0:T(8,128)(2,1)} %collective-permute-done.33), channel_id=1, source_target_pairs={{0,8},{4,12},{8,16},{12,20},{16,24},{20,28},{24,0},{28,4},{1,9},{5... | collective-permute-start | bytes 884744 | tf_op jit(solution)/shard_map/ppermute | solution.py:74
  180.9 23.9 %collective-permute-start.55 = (bf16[128,1152]{1,0:T(8,128)(2,1)}, bf16[128,1152]{1,0:T(8,128)(2,1)S(1)}, u32[]{:S(2)}, u32[]{:S(2)}) collective-permute-start(bf16[128,1152]{1,0:T(8,128)(2,1)} %collective-permute-done.53), channel_id=1, source_target_pairs={{0,8},{4,12},{8,16},{12,20},{16,24},{20,28},{24,0},{28,4},{1,9},{5... | collective-permute-start | bytes 884744 | tf_op jit(solution)/shard_map/ppermute | solution.py:74
  194.9 11.4 %collective-permute-start.21 = (bf16[256,1024]{1,0:T(8,128)(2,1)S(1)}, bf16[256,1024]{1,0:T(8,128)(2,1)S(1)}, u32[]{:S(2)}, u32[]{:S(2)}) collective-permute-start(bf16[256,1024]{1,0:T(8,128)(2,1)S(1)} %get-tuple-element.50), channel_id=1, source_target_pairs={{0,1},{1,0},{2,3},{3,2},{4,5},{5,4},{6,7},{7,6},{8,9},{9,8},{10,11... | collective-permute-start | bytes 1572872 | tf_op jit(solution)/shard_map/ppermute | solution.py:42
  195.2 14.4 %collective-permute-start.23 = (bf16[256,1024]{1,0:T(8,128)(2,1)S(1)}, bf16[256,1024]{1,0:T(8,128)(2,1)S(1)}, u32[]{:S(2)}, u32[]{:S(2)}) collective-permute-start(bf16[256,1024]{1,0:T(8,128)(2,1)S(1)} %add_convert_fusion.5), channel_id=1, source_target_pairs={{0,2},{1,3},{2,0},{3,1},{4,6},{5,7},{6,4},{7,5},{8,10},{9,11},{10,... | collective-permute-start | bytes 1572872 | tf_op jit(solution)/shard_map/ppermute | solution.py:42
  204.8 23.1 %collective-permute-start.36 = (bf16[128,1152]{1,0:T(8,128)(2,1)S(1)}, bf16[128,1152]{1,0:T(8,128)(2,1)S(1)}, u32[]{:S(2)}, u32[]{:S(2)}) collective-permute-start(bf16[128,1152]{1,0:T(8,128)(2,1)S(1)} %collective-permute-done.35), channel_id=1, source_target_pairs={{0,4},{4,0},{8,12},{12,8},{16,20},{20,16},{24,28},{28,24},{1,5},{5... | collective-permute-start | bytes 884744 | tf_op jit(solution)/shard_map/ppermute | solution.py:42
  206.4 21.4 %collective-permute-start.56 = (bf16[128,1152]{1,0:T(8,128)(2,1)S(1)}, bf16[128,1152]{1,0:T(8,128)(2,1)S(1)}, u32[]{:S(2)}, u32[]{:S(2)}) collective-permute-start(bf16[128,1152]{1,0:T(8,128)(2,1)S(1)} %collective-permute-done.55), channel_id=1, source_target_pairs={{0,4},{4,0},{8,12},{12,8},{16,20},{20,16},{24,28},{28,24},{1,5},{5... | collective-permute-start | bytes 884744 | tf_op jit(solution)/shard_map/ppermute | solution.py:42
  209.6 16.4 %collective-permute-start.46 = (bf16[128,1152]{1,0:T(8,128)(2,1)}, bf16[128,1152]{1,0:T(8,128)(2,1)S(1)}, u32[]{:S(2)}, u32[]{:S(2)}) collective-permute-start(bf16[128,1152]{1,0:T(8,128)(2,1)} %collective-permute-done.45), channel_id=1, source_target_pairs={{0,4},{4,0},{8,12},{12,8},{16,20},{20,16},{24,28},{28,24},{1,5},{5... | collective-permute-start | bytes 884744 | tf_op jit(solution)/shard_map/ppermute | solution.py:42
  226.0 12.7 %collective-permute-start.25 = (bf16[256,1024]{1,0:T(8,128)(2,1)S(1)}, bf16[256,1024]{1,0:T(8,128)(2,1)S(1)}, u32[]{:S(2)}, u32[]{:S(2)}) collective-permute-start(bf16[256,1024]{1,0:T(8,128)(2,1)S(1)} %multiply_convert_fusion.2), channel_id=1, source_target_pairs={{0,2},{1,3},{2,0},{3,1},{4,6},{5,7},{6,4},{7,5},{8,10},{9,11},{10,... | collective-permute-start | bytes 1572872 | tf_op jit(solution)/shard_map/ppermute | solution.py:42
  227.9 15.2 %collective-permute-start.24 = (bf16[256,1024]{1,0:T(8,128)(2,1)S(1)}, bf16[256,1024]{1,0:T(8,128)(2,1)S(1)}, u32[]{:S(2)}, u32[]{:S(2)}) collective-permute-start(bf16[256,1024]{1,0:T(8,128)(2,1)S(1)} %multiply_convert_fusion.2), channel_id=1, source_target_pairs={{0,1},{1,0},{2,3},{3,2},{4,5},{5,4},{6,7},{7,6},{8,9},{9,8},{10,11... | collective-permute-start | bytes 1572872 | tf_op jit(solution)/shard_map/ppermute | solution.py:42
  259.1 102.7 %collective-permute-start.57 = (bf16[256,1024]{1,0:T(8,128)(2,1)S(1)}, bf16[256,1024]{1,0:T(8,128)(2,1)S(1)}, u32[]{:S(2)}, u32[]{:S(2)}) collective-permute-start(bf16[256,1024]{1,0:T(8,128)(2,1)S(1)} %get-tuple-element.48), channel_id=1, source_target_pairs={{0,1},{1,0},{2,3},{3,2},{4,5},{5,4},{6,7},{7,6},{8,9},{9,8},{10,11... | collective-permute-start | bytes 1572872 | tf_op jit(solution)/shard_map/ppermute | solution.py:42
  259.7 41.5 %collective-permute-start.58 = (bf16[256,1024]{1,0:T(8,128)(2,1)S(1)}, bf16[256,1024]{1,0:T(8,128)(2,1)S(1)}, u32[]{:S(2)}, u32[]{:S(2)}) collective-permute-start(bf16[256,1024]{1,0:T(8,128)(2,1)S(1)} %get-tuple-element.49), channel_id=1, source_target_pairs={{0,1},{1,0},{2,3},{3,2},{4,5},{5,4},{6,7},{7,6},{8,9},{9,8},{10,11... | collective-permute-start | bytes 1572872 | tf_op jit(solution)/shard_map/ppermute | solution.py:42
  264.3 19.9 %collective-permute-start.105 = (bf16[128,1152]{1,0:T(8,128)(2,1)S(1)}, bf16[128,1152]{1,0:T(8,128)(2,1)S(1)}, u32[]{:S(2)}, u32[]{:S(2)}) collective-permute-start(bf16[128,1152]{1,0:T(8,128)(2,1)S(1)} %get-tuple-element.33), channel_id=1, source_target_pairs={{0,4},{4,0},{8,12},{12,8},{16,20},{20,16},{24,28},{28,24},{1,5},{5... | collective-permute-start | bytes 884744 | tf_op jit(solution)/shard_map/ppermute | solution.py:42
  266.0 37.4 %collective-permute-start.104 = (bf16[128,1152]{1,0:T(8,128)(2,1)S(1)}, bf16[128,1152]{1,0:T(8,128)(2,1)S(1)}, u32[]{:S(2)}, u32[]{:S(2)}) collective-permute-start(bf16[128,1152]{1,0:T(8,128)(2,1)S(1)} %get-tuple-element.34), channel_id=1, source_target_pairs={{0,4},{4,0},{8,12},{12,8},{16,20},{20,16},{24,28},{28,24},{1,5},{5... | collective-permute-start | bytes 884744 | tf_op jit(solution)/shard_map/ppermute | solution.py:42
  266.4 66.2 %collective-permute-start.103 = (bf16[128,1152]{1,0:T(8,128)(2,1)S(1)}, bf16[128,1152]{1,0:T(8,128)(2,1)S(1)}, u32[]{:S(2)}, u32[]{:S(2)}) collective-permute-start(bf16[128,1152]{1,0:T(8,128)(2,1)S(1)} %get-tuple-element.35), channel_id=1, source_target_pairs={{0,4},{4,0},{8,12},{12,8},{16,20},{20,16},{24,28},{28,24},{1,5},{5... | collective-permute-start | bytes 884744 | tf_op jit(solution)/shard_map/ppermute | solution.py:42
  301.2 11.3 %collective-permute-start.106 = (bf16[128,1152]{1,0:T(8,128)(2,1)S(1)}, bf16[128,1152]{1,0:T(8,128)(2,1)S(1)}, u32[]{:S(2)}, u32[]{:S(2)}) collective-permute-start(bf16[128,1152]{1,0:T(8,128)(2,1)S(1)} %add_convert_fusion.9), channel_id=1, source_target_pairs={{0,8},{4,12},{8,16},{12,20},{16,24},{20,28},{24,0},{28,4},{1,9},{5... | collective-permute-start | bytes 884744 | tf_op jit(solution)/shard_map/ppermute | solution.py:74
  303.0 56.2 %collective-permute-start.63 = (bf16[256,1024]{1,0:T(8,128)(2,1)S(1)}, bf16[256,1024]{1,0:T(8,128)(2,1)S(1)}, u32[]{:S(2)}, u32[]{:S(2)}) collective-permute-start(bf16[256,1024]{1,0:T(8,128)(2,1)S(1)} %get-tuple-element.46), channel_id=1, source_target_pairs={{0,1},{1,0},{2,3},{3,2},{4,5},{5,4},{6,7},{7,6},{8,9},{9,8},{10,11... | collective-permute-start | bytes 1572872 | tf_op jit(solution)/shard_map/ppermute | solution.py:42
  312.5 10.4 %collective-permute-start.96 = (bf16[128,1152]{1,0:T(8,128)(2,1)S(1)}, bf16[128,1152]{1,0:T(8,128)(2,1)S(1)}, u32[]{:S(2)}, u32[]{:S(2)}) collective-permute-start(bf16[128,1152]{1,0:T(8,128)(2,1)S(1)} %add_convert_fusion.13), channel_id=1, source_target_pairs={{0,8},{4,12},{8,16},{12,20},{16,24},{20,28},{24,0},{28,4},{1,9},{5... | collective-permute-start | bytes 884744 | tf_op jit(solution)/shard_map/ppermute | solution.py:74
  312.7 10.3 %collective-permute-start.84 = (bf16[128,1152]{1,0:T(8,128)(2,1)S(1)}, bf16[128,1152]{1,0:T(8,128)(2,1)S(1)}, u32[]{:S(2)}, u32[]{:S(2)}) collective-permute-start(bf16[128,1152]{1,0:T(8,128)(2,1)S(1)} %get-tuple-element.42), channel_id=1, source_target_pairs={{0,4},{4,0},{8,12},{12,8},{16,20},{20,16},{24,28},{28,24},{1,5},{5... | collective-permute-start | bytes 884744 | tf_op jit(solution)/shard_map/ppermute | solution.py:42
  322.9 9.5 %collective-permute-start.86 = (bf16[128,1152]{1,0:T(8,128)(2,1)S(1)}, bf16[128,1152]{1,0:T(8,128)(2,1)S(1)}, u32[]{:S(2)}, u32[]{:S(2)}) collective-permute-start(bf16[128,1152]{1,0:T(8,128)(2,1)S(1)} %add_convert_fusion.17), channel_id=1, source_target_pairs={{0,8},{4,12},{8,16},{12,20},{16,24},{20,28},{24,0},{28,4},{1,9},{5... | collective-permute-start | bytes 884744 | tf_op jit(solution)/shard_map/ppermute | solution.py:74
  323.0 18.2 %collective-permute-start.93 = (bf16[128,1152]{1,0:T(8,128)(2,1)S(1)}, bf16[128,1152]{1,0:T(8,128)(2,1)S(1)}, u32[]{:S(2)}, u32[]{:S(2)}) collective-permute-start(bf16[128,1152]{1,0:T(8,128)(2,1)S(1)} %get-tuple-element.39), channel_id=1, source_target_pairs={{0,4},{4,0},{8,12},{12,8},{16,20},{20,16},{24,28},{28,24},{1,5},{5... | collective-permute-start | bytes 884744 | tf_op jit(solution)/shard_map/ppermute | solution.py:42
  332.6 17.1 %collective-permute-start.83 = (bf16[128,1152]{1,0:T(8,128)(2,1)S(1)}, bf16[128,1152]{1,0:T(8,128)(2,1)S(1)}, u32[]{:S(2)}, u32[]{:S(2)}) collective-permute-start(bf16[128,1152]{1,0:T(8,128)(2,1)S(1)} %get-tuple-element.43), channel_id=1, source_target_pairs={{0,4},{4,0},{8,12},{12,8},{16,20},{20,16},{24,28},{28,24},{1,5},{5... | collective-permute-start | bytes 884744 | tf_op jit(solution)/shard_map/ppermute | solution.py:42
  341.2 19.8 %collective-permute-start.65 = (bf16[256,1024]{1,0:T(8,128)(2,1)S(1)}, bf16[256,1024]{1,0:T(8,128)(2,1)S(1)}, u32[]{:S(2)}, u32[]{:S(2)}) collective-permute-start(bf16[256,1024]{1,0:T(8,128)(2,1)S(1)} %add_convert_fusion.2), channel_id=1, source_target_pairs={{0,2},{1,3},{2,0},{3,1},{4,6},{5,7},{6,4},{7,5},{8,10},{9,11},{10,... | collective-permute-start | bytes 1572872 | tf_op jit(solution)/shard_map/ppermute | solution.py:42
  349.7 21.3 %collective-permute-start.102 = (bf16[128,1152]{1,0:T(8,128)(2,1)S(1)}, bf16[128,1152]{1,0:T(8,128)(2,1)S(1)}, u32[]{:S(2)}, u32[]{:S(2)}) collective-permute-start(bf16[128,1152]{1,0:T(8,128)(2,1)S(1)} %get-tuple-element.32), channel_id=1, source_target_pairs={{0,4},{4,0},{8,12},{12,8},{16,20},{20,16},{24,28},{28,24},{1,5},{5... | collective-permute-start | bytes 884744 | tf_op jit(solution)/shard_map/ppermute | solution.py:42
  358.1 10.4 %collective-permute-start.59 = (bf16[256,1024]{1,0:T(8,128)(2,1)S(1)}, bf16[256,1024]{1,0:T(8,128)(2,1)S(1)}, u32[]{:S(2)}, u32[]{:S(2)}) collective-permute-start(bf16[256,1024]{1,0:T(8,128)(2,1)S(1)} %add_convert_fusion.4), channel_id=1, source_target_pairs={{0,2},{1,3},{2,0},{3,1},{4,6},{5,7},{6,4},{7,5},{8,10},{9,11},{10,... | collective-permute-start | bytes 1572872 | tf_op jit(solution)/shard_map/ppermute | solution.py:42
  359.3 15.6 %collective-permute-start.92 = (bf16[128,1152]{1,0:T(8,128)(2,1)S(1)}, bf16[128,1152]{1,0:T(8,128)(2,1)S(1)}, u32[]{:S(2)}, u32[]{:S(2)}) collective-permute-start(bf16[128,1152]{1,0:T(8,128)(2,1)S(1)} %get-tuple-element.36), channel_id=1, source_target_pairs={{0,4},{4,0},{8,12},{12,8},{16,20},{20,16},{24,28},{28,24},{1,5},{5... | collective-permute-start | bytes 884744 | tf_op jit(solution)/shard_map/ppermute | solution.py:42
  361.1 18.3 %collective-permute-start.82 = (bf16[128,1152]{1,0:T(8,128)(2,1)S(1)}, bf16[128,1152]{1,0:T(8,128)(2,1)S(1)}, u32[]{:S(2)}, u32[]{:S(2)}) collective-permute-start(bf16[128,1152]{1,0:T(8,128)(2,1)S(1)} %get-tuple-element.40), channel_id=1, source_target_pairs={{0,4},{4,0},{8,12},{12,8},{16,20},{20,16},{24,28},{28,24},{1,5},{5... | collective-permute-start | bytes 884744 | tf_op jit(solution)/shard_map/ppermute | solution.py:42
  361.8 11.8 %collective-permute-start.108 = (bf16[128,1152]{1,0:T(8,128)(2,1)S(1)}, bf16[128,1152]{1,0:T(8,128)(2,1)S(1)}, u32[]{:S(2)}, u32[]{:S(2)}) collective-permute-start(bf16[128,1152]{1,0:T(8,128)(2,1)S(1)} %add_convert_fusion.7), channel_id=1, source_target_pairs={{0,8},{4,12},{8,16},{12,20},{16,24},{20,28},{24,0},{28,4},{1,9},{5... | collective-permute-start | bytes 884744 | tf_op jit(solution)/shard_map/ppermute | solution.py:74
  371.0 10.0 %collective-permute-start.88 = (bf16[128,1152]{1,0:T(8,128)(2,1)S(1)}, bf16[128,1152]{1,0:T(8,128)(2,1)S(1)}, u32[]{:S(2)}, u32[]{:S(2)}) collective-permute-start(bf16[128,1152]{1,0:T(8,128)(2,1)S(1)} %add_convert_fusion.15), channel_id=1, source_target_pairs={{0,8},{4,12},{8,16},{12,20},{16,24},{20,28},{24,0},{28,4},{1,9},{5... | collective-permute-start | bytes 884744 | tf_op jit(solution)/shard_map/ppermute | solution.py:74
  373.6 18.5 %collective-permute-start.67 = (bf16[256,1024]{1,0:T(8,128)(2,1)S(1)}, bf16[256,1024]{1,0:T(8,128)(2,1)S(1)}, u32[]{:S(2)}, u32[]{:S(2)}) collective-permute-start(bf16[256,1024]{1,0:T(8,128)(2,1)S(1)} %get-tuple-element.23), channel_id=1, source_target_pairs={{0,2},{1,3},{2,0},{3,1},{4,6},{5,7},{6,4},{7,5},{8,10},{9,11},{10,... | collective-permute-start | bytes 1572872 | tf_op jit(solution)/shard_map/ppermute | solution.py:42
  374.9 20.5 %collective-permute-start.66 = (bf16[256,1024]{1,0:T(8,128)(2,1)S(1)}, bf16[256,1024]{1,0:T(8,128)(2,1)S(1)}, u32[]{:S(2)}, u32[]{:S(2)}) collective-permute-start(bf16[256,1024]{1,0:T(8,128)(2,1)S(1)} %get-tuple-element.23), channel_id=1, source_target_pairs={{0,1},{1,0},{2,3},{3,2},{4,5},{5,4},{6,7},{7,6},{8,9},{9,8},{10,11... | collective-permute-start | bytes 1572872 | tf_op jit(solution)/shard_map/ppermute | solution.py:42
  388.5 58.2 %collective-permute-start.91 = (bf16[32,1152]{1,0:T(8,128)(2,1)S(1)}, bf16[32,1152]{1,0:T(8,128)(2,1)S(1)}, u32[]{:S(2)}, u32[]{:S(2)}) collective-permute-start(bf16[32,1152]{1,0:T(8,128)(2,1)S(1)} %get-tuple-element.73), channel_id=1, source_target_pairs={{0,3},{1,2},{2,1},{3,0},{4,7},{5,6},{6,5},{7,4},{8,11},{9,10},{10,... | collective-permute-start | bytes 221192 | tf_op jit(solution)/shard_map/ppermute | solution.py:42
  447.4 32.3 %collective-permute-start.72 = (bf16[128,768]{0,1:T(8,128)(2,1)}, bf16[128,768]{0,1:T(8,128)(2,1)S(1)}, u32[]{:S(2)}, u32[]{:S(2)}) collective-permute-start(bf16[128,768]{0,1:T(8,128)(2,1)} %get-tuple-element.52), channel_id=1, source_target_pairs={{0,4},{4,0},{8,12},{12,8},{16,20},{20,16},{24,28},{28,24},{1,5},{5... | collective-permute-start | bytes 589832 | tf_op jit(solution)/shard_map/ppermute | solution.py:42
  449.2 18.6 %collective-permute-start.73 = (bf16[128,768]{0,1:T(8,128)(2,1)}, bf16[128,768]{0,1:T(8,128)(2,1)S(1)}, u32[]{:S(2)}, u32[]{:S(2)}) collective-permute-start(bf16[128,768]{0,1:T(8,128)(2,1)} %get-tuple-element.53), channel_id=1, source_target_pairs={{0,4},{4,0},{8,12},{12,8},{16,20},{20,16},{24,28},{28,24},{1,5},{5... | collective-permute-start | bytes 589832 | tf_op jit(solution)/shard_map/ppermute | solution.py:42
  449.4 14.7 %collective-permute-start.74 = (bf16[128,768]{0,1:T(8,128)(2,1)}, bf16[128,768]{0,1:T(8,128)(2,1)}, u32[]{:S(2)}, u32[]{:S(2)}) collective-permute-start(bf16[128,768]{0,1:T(8,128)(2,1)} %get-tuple-element.54), channel_id=1, source_target_pairs={{0,4},{4,0},{8,12},{12,8},{16,20},{20,16},{24,28},{28,24},{1,5},{5... | collective-permute-start | bytes 589832 | tf_op jit(solution)/shard_map/ppermute | solution.py:42
  458.3 43.8 %collective-permute-start.69 = (bf16[256,1024]{1,0:T(8,128)(2,1)}, bf16[256,1024]{1,0:T(8,128)(2,1)}, u32[]{:S(2)}, u32[]{:S(2)}) collective-permute-start(bf16[256,1024]{1,0:T(8,128)(2,1)} %get-tuple-element.44), channel_id=1, source_target_pairs={{0,1},{1,0},{2,3},{3,2},{4,5},{5,4},{6,7},{7,6},{8,9},{9,8},{10,11... | collective-permute-start | bytes 1572872 | tf_op jit(solution)/shard_map/ppermute | solution.py:42
  464.1 12.3 %collective-permute-start.70 = (bf16[256,1024]{1,0:T(8,128)(2,1)}, bf16[256,1024]{1,0:T(8,128)(2,1)}, u32[]{:S(2)}, u32[]{:S(2)}) collective-permute-start(bf16[256,1024]{1,0:T(8,128)(2,1)} %get-tuple-element.45), channel_id=1, source_target_pairs={{0,1},{1,0},{2,3},{3,2},{4,5},{5,4},{6,7},{7,6},{8,9},{9,8},{10,11... | collective-permute-start | bytes 1572872 | tf_op jit(solution)/shard_map/ppermute | solution.py:42
  478.6 23.6 %collective-permute-start.71 = (bf16[256,1024]{1,0:T(8,128)(2,1)}, bf16[256,1024]{1,0:T(8,128)(2,1)}, u32[]{:S(2)}, u32[]{:S(2)}) collective-permute-start(bf16[256,1024]{1,0:T(8,128)(2,1)} %add_convert_fusion.1), channel_id=1, source_target_pairs={{0,2},{1,3},{2,0},{3,1},{4,6},{5,7},{6,4},{7,5},{8,10},{9,11},{10,... | collective-permute-start | bytes 1572872 | tf_op jit(solution)/shard_map/ppermute | solution.py:42
  485.6 10.9 %collective-permute-start.81 = (bf16[32,768]{0,1:T(8,128)(2,1)S(1)}, bf16[32,768]{0,1:T(8,128)(2,1)S(1)}, u32[]{:S(2)}, u32[]{:S(2)}) collective-permute-start(bf16[32,768]{0,1:T(8,128)(2,1)S(1)} %get-tuple-element.104), channel_id=1, source_target_pairs={{0,3},{1,2},{2,1},{3,0},{4,7},{5,6},{6,5},{7,4},{8,11},{9,10},{10,... | collective-permute-start | bytes 147464 | tf_op jit(solution)/shard_map/ppermute | solution.py:42
  485.7 15.1 %collective-permute-start.80 = (bf16[32,768]{0,1:T(8,128)(2,1)S(1)}, bf16[32,768]{0,1:T(8,128)(2,1)S(1)}, u32[]{:S(2)}, u32[]{:S(2)}) collective-permute-start(bf16[32,768]{0,1:T(8,128)(2,1)S(1)} %get-tuple-element.105), channel_id=1, source_target_pairs={{0,2},{1,3},{2,0},{3,1},{4,6},{5,7},{6,4},{7,5},{8,10},{9,11},{10,... | collective-permute-start | bytes 147464 | tf_op jit(solution)/shard_map/ppermute | solution.py:42
  486.8 14.7 %collective-permute-start.79 = (bf16[32,768]{0,1:T(8,128)(2,1)S(1)}, bf16[32,768]{0,1:T(8,128)(2,1)S(1)}, u32[]{:S(2)}, u32[]{:S(2)}) collective-permute-start(bf16[32,768]{0,1:T(8,128)(2,1)S(1)} %get-tuple-element.106), channel_id=1, source_target_pairs={{0,1},{1,0},{2,3},{3,2},{4,5},{5,4},{6,7},{7,6},{8,9},{9,8},{10,11... | collective-permute-start | bytes 147464 | tf_op jit(solution)/shard_map/ppermute | solution.py:42
  (112 other events, 1190.1 us)
